TPU v7x, 256 devices: a whole 4x4x8 slice. The times are simulated.
256 devices in a mesh: seq: 16 (over z, y_lo), res: 16 (over y_hi, x, core).
Axes of the slice: x: 4, y: 4 (y_hi: 2, y_lo: 2; y = y_hi * 2 + y_lo), z: 8, core: 2. Of those that a mesh axis runs over, the one named last changes fastest.
Arguments:
- target_alignment_matrix: float32 [1024, 128, 256], P('seq', 'res'), may hold values from -6 to 6
- source_alignment_matrix: float32 [1024, 128, 256], P('seq', 'res'), may hold values from -6 to 6
- source_mapping_matrix: float32 [256, 32], replicated, may hold values from -0.375 to 0.375
- target_mapping_matrix: float32 [256, 32], replicated, may hold values from -0.375 to 0.375
- final_mapping_matrix: float32 [1024, 128], replicated, may hold values from -6 to 6
- edge_offset_vector: float32 [128], replicated, may hold values from -3 to 3
- edge_delta_cotangent: float32 [128, 128, 128], P('seq', 'res'), may hold values from -6 to 6
Outputs:
- edge_delta_result: float32 [128, 128, 128], P('seq', 'res')
- grad_cols: float32 [1024, 128, 256], P('seq', 'res')
- grad_rows: float32 [1024, 128, 256], P('seq', 'res')
- grad_left: float32 [256, 32], replicated
- grad_right: float32 [256, 32], replicated
- grad_proj: float32 [1024, 128], replicated
- grad_bias: float32 [128], replicated
All inputs are finite; a program needn't handle non-finite values.
Results may differ from a plain program's by a relative error of at most 0.00013.
Values sent between devices are 32-bit elements; how exact they have to be, the bound alone decides.
A program may use at most 64 MiB of HBM per device.

v0:
```python
import jax
import jax.numpy as jnp
from jax import lax
from jax.sharding import PartitionSpec as P


def standardize_features(values):
    average = jnp.mean(values, axis=-1, keepdims=True)
    centred = values - average
    inverse = lax.rsqrt(jnp.mean(centred * centred, axis=-1, keepdims=True) + 1e-05)
    return (centred * inverse, inverse)


def normalize_back(normed, inverse, upstream):
    first = jnp.mean(upstream, axis=-1, keepdims=True)
    second = jnp.mean(upstream * normed, axis=-1, keepdims=True)
    return inverse * (upstream - first - normed * second)


def body(
    target_alignment_matrix,
    source_alignment_matrix,
    source_mapping_matrix,
    target_mapping_matrix,
    final_mapping_matrix,
    edge_offset_vector,
    edge_delta_cotangent,
):
    exact_arithmetic = lax.Precision.HIGHEST
    member_tally, amino_tally, feature_tally = target_alignment_matrix.shape
    hidden = source_mapping_matrix.shape[1]
    square = hidden * hidden
    pair_width = final_mapping_matrix.shape[1]
    seqs_total = member_tally * lax.axis_size("seq")
    own_rows = edge_delta_cotangent.shape[0]
    source_scaling_divisor, source_inverted_scale = standardize_features(source_alignment_matrix)
    target_scaling_divisor, target_inverted_scale = standardize_features(target_alignment_matrix)
    left_rows = jnp.einsum(
        "uwh,hq->uwq", source_scaling_divisor, source_mapping_matrix, precision=exact_arithmetic
    )
    right_cols = jnp.einsum(
        "iwe,ed->iwd", target_scaling_divisor, target_mapping_matrix, precision=exact_arithmetic
    )
    left_full = lax.all_gather(left_rows, "res", axis=1, tiled=True)
    slab_rows = left_full.shape[1]
    partial_value = (
        jnp.einsum("ipu,ihl->phul", left_full, right_cols, precision=exact_arithmetic) / seqs_total
    )
    partial_value = partial_value.reshape(slab_rows, amino_tally, square)
    flat_grad = edge_delta_cotangent.reshape(own_rows * amino_tally, pair_width)
    reduced = lax.psum_scatter(partial_value, "seq", scatter_dimension=0, tiled=True)
    reduced_flat = reduced.reshape(own_rows * amino_tally, square)
    edge_delta_result = (
        jnp.dot(reduced_flat, final_mapping_matrix, precision=exact_arithmetic).reshape(
            own_rows, amino_tally, pair_width
        )
        + edge_offset_vector
    )
    local_grad = jnp.dot(flat_grad, final_mapping_matrix.T, precision=exact_arithmetic).reshape(
        own_rows, amino_tally, square
    )
    grad_full = lax.all_gather(local_grad, "seq", axis=0, tiled=True)
    grad_out = jnp.einsum("pa,pb->ab", reduced_flat, flat_grad, precision=exact_arithmetic)
    grad_four = grad_full.reshape(slab_rows, amino_tally, hidden, hidden)
    grad_left_part = (
        jnp.einsum("ijhk,sjk->sih", grad_four, right_cols, precision=exact_arithmetic) / seqs_total
    )
    grad_right_side = (
        jnp.einsum("ijhk,sih->sjk", grad_four, left_full, precision=exact_arithmetic) / seqs_total
    )
    grad_left_side = lax.psum_scatter(grad_left_part, "res", scatter_dimension=1, tiled=True)
    grad_wleft = jnp.einsum(
        "sic,sih->ch", source_scaling_divisor, grad_left_side, precision=exact_arithmetic
    )
    grad_wright = jnp.einsum(
        "sjc,sjh->ch", target_scaling_divisor, grad_right_side, precision=exact_arithmetic
    )
    grad_bpart = jnp.sum(flat_grad, axis=0)
    grad_left, grad_right, grad_proj, grad_bias = lax.psum(
        (grad_wleft, grad_wright, grad_out, grad_bpart), ("seq", "res")
    )
    upstream_rows = jnp.einsum(
        "sih,ch->sic", grad_left_side, source_mapping_matrix, precision=exact_arithmetic
    )
    upstream_cols = jnp.einsum(
        "sjh,ch->sjc", grad_right_side, target_mapping_matrix, precision=exact_arithmetic
    )
    grad_rows = normalize_back(source_scaling_divisor, source_inverted_scale, upstream_rows)
    grad_cols = normalize_back(target_scaling_divisor, target_inverted_scale, upstream_cols)
    return (edge_delta_result, grad_cols, grad_rows, grad_left, grad_right, grad_proj, grad_bias)


def solution(mesh):
    in_specs = (
        P("seq", "res", None),
        P("seq", "res", None),
        P(),
        P(),
        P(),
        P(),
        P("seq", "res", None),
    )
    out_specs = (
        P("seq", "res", None),
        P("seq", "res", None),
        P("seq", "res", None),
        P(),
        P(),
        P(),
        P(),
    )
    return jax.shard_map(body, mesh=mesh, in_specs=in_specs, out_specs=out_specs, check_vma=False)
```

profile of v0, /device:TPU:1, one launch (start us, length us, event | category | flops | bytes accessed | tf_op | source)
XLA Modules:
  0.0 882.4 jit_solution(16809121184989202640)
XLA Ops:
  7.2 0.0 copy-start
  7.2 0.0 copy-start.1
  7.2 0.0 copy-start.4
  7.2 0.0 all-gather.5.cloned.1.call-start
  7.3 1.0 copy-done
  8.2 2.1 fusion.9
  10.3 0.0 all-gather.5.cloned.1.call-update
  10.4 0.0 all-gather.3.cloned.1.call-start
  10.4 1.2 reduce_sum.83
  11.6 1.3 multiply_reduce_fusion.2
  12.9 2.4 fusion.13
  15.3 0.0 all-gather.3.cloned.1.call-update
  15.3 0.0 reduce-scatter.5.cloned.1.call-start
  15.4 1.2 reduce_sum.81
  16.6 0.0 copy-done.1
  16.6 0.2 multiply_reduce_fusion.3
  16.8 0.0 copy-done.4
  16.9 0.6 fusion.12
  17.5 0.1 copy.44
  17.6 93.4 %all-gather.5.cloned.1.call-done = f32[128,8,1024]{2,1,0:T(8,128)} async-done(((f32[8,8,1024]{2,1,0:T(8,128)}), f32[128,8,1024]{2,1,0:T(8,128)}) %all-gather.5.cloned.1.call-update) | async-done | bytes 4194320 | tf_op jit(solution)/shard_map/all_gather | solution.py:62
  111.0 5.4 copy.41
  116.4 10.2 %bitcast_multiply_fusion = f32[64,128,32]{0,1,2:T(8,128)} fusion(f32[128,8,32,32]{0,3,2,1:T(8,128)} %bitcast.65, f32[64,8,32]{0,2,1:T(8,128)S(1)} %copy.44), kind=kOutput, calls=%fused_computation.1 | convolution fusion | flops 805568512 | bytes 5308416 | tf_op jit(solution)/shard_map/ijhk,sjk->sih/dot_general | solution.py:66
  126.7 0.0 reduce-scatter.5.cloned.1.call-update
  126.7 0.2 reduce-scatter.3.cloned.1.call-start
  126.9 53.7 %all-gather.3.cloned.1.call-done = f32[64,128,32]{2,1,0:T(8,128)} async-done(((f32[64,8,32]{2,1,0:T(8,128)}), f32[64,128,32]{2,1,0:T(8,128)}) %all-gather.3.cloned.1.call-update) | async-done | bytes 1048592 | tf_op jit(solution)/shard_map/all_gather | solution.py:44
  180.6 4.4 copy.39
  185.0 8.2 convolution_multiply_fusion
  193.1 5.6 copy.40
  198.8 0.0 copy-start.3
  198.8 0.0 reduce-scatter.3.cloned.1.call-update
  198.8 0.0 copy-start.5
  198.8 0.0 all-reduce.6.cloned.1.call-start
  198.9 0.7 copy-done.3
  199.5 0.5 reduce_sum.89
  200.1 6.8 fusion.6
  206.8 0.0 copy-start.2
  206.8 0.0 copy-start.6
  206.8 0.1 copy.43
  207.0 1.4 convolution_bitcast_fusion.1
  208.4 0.0 copy-done.5
  208.4 0.6 fusion.31
  209.0 0.0 copy-start.7
  209.0 1.1 subtract_multiply_fusion.1
  210.2 49.6 %reduce-scatter.5.cloned.1.call-done = f32[64,8,32]{0,1,2:T(8,128)} async-done(((f32[64,128,32]{0,1,2:T(8,128)}), f32[64,8,32]{0,1,2:T(8,128)}) %reduce-scatter.5.cloned.1.call-update) | async-done | bytes 65552 | tf_op jit(solution)/shard_map/reduce_scatter | solution.py:71
  259.8 1.1 copy.46
  260.8 0.0 copy-done.2
  260.8 1.4 convolution_bitcast_fusion.2
  262.2 0.0 copy-done.6
  262.2 0.6 fusion.30
  262.8 0.0 all-reduce.6.cloned.1.call-update
  262.9 0.0 all-reduce.4.cloned.1.call-start
  262.9 98.3 %reduce-scatter.3.cloned.1.call-done = f32[8,8,1024]{2,1,0:T(8,128)} async-done(((f32[128,8,1024]{2,1,0:T(8,128)}), f32[8,8,1024]{2,1,0:T(8,128)}) %reduce-scatter.3.cloned.1.call-update) | async-done | bytes 262160 | tf_op jit(solution)/shard_map/reduce_scatter | solution.py:51
  361.2 2.7 convolution_bitcast_fusion
  364.0 0.0 all-reduce.4.cloned.1.call-update
  364.0 1.1 subtract_multiply_fusion
  365.1 0.0 copy-done.7
  365.1 2.0 convolution_add_fusion
  367.1 246.7 %all-reduce.6.cloned.1.call-done = (f32[256,32]{0,1:T(8,128)}, f32[256,32]{0,1:T(8,128)}, f32[128]{0:T(128)}) async-done(((f32[256,32]{0,1:T(8,128)}, f32[256,32]{0,1:T(8,128)}, f32[128]{0:T(128)}), (f32[256,32]{0,1:T(8,128)}, f32[256,32]{0,1:T(8,128)}, f32[128]{0:T(128)})) %all-reduce.6.cloned.1.call-update) | async-done | bytes 66064 | tf_op jit(solution)/shard_map/psum | solution.py:79
  613.8 256.0 %all-reduce.4.cloned.1.call-done = f32[1024,128]{1,0:T(8,128)} async-done(((f32[1024,128]{1,0:T(8,128)}), f32[1024,128]{1,0:T(8,128)}) %all-reduce.4.cloned.1.call-update) | async-done | bytes 524304 | tf_op jit(solution)/shard_map/psum | solution.py:79
  869.8 1.4 copy.60
  871.2 1.4 copy.61
  872.6 1.9 copy.62
  874.4 1.1 copy.63
  (6 shorter events, 0.1 us)
Async XLA Ops:
  7.2 1.0 copy-start
  7.2 9.4 %copy-start.1 = (f32[64,8,256]{2,1,0:T(8,128)S(1)}, f32[64,8,256]{2,1,0:T(8,128)}, u32[]{:S(2)}) copy-start(f32[64,8,256]{2,1,0:T(8,128)} %param.7) | copy-start | bytes 1572868
  7.2 9.6 %copy-start.4 = (f32[256,32]{0,1:T(8,128)S(1)}, f32[256,32]{0,1:T(8,128)}, u32[]{:S(2)}) copy-start(f32[256,32]{0,1:T(8,128)} %param.10) | copy-start | bytes 98308
  7.2 103.8 %all-gather.5.cloned.1.call-start = ((), (), s32[]{:S(2)}) async-start(), calls=%async_computation.4 | async-start | bytes 4456448 | tf_op jit(solution)/shard_map/all_gather | solution.py:62
  10.4 170.2 %all-gather.3.cloned.1.call-start = ((), (), s32[]{:S(2)}) async-start(), calls=%async_computation.2 | async-start | bytes 4456448 | tf_op jit(solution)/shard_map/all_gather | solution.py:44
  15.3 244.4 %reduce-scatter.5.cloned.1.call-start = ((), (), s32[]{:S(2)}) async-start(), calls=%async_computation.5 | async-start | bytes 2228224 | tf_op jit(solution)/shard_map/reduce_scatter | solution.py:71
  126.7 234.5 %reduce-scatter.3.cloned.1.call-start = ((), (), s32[]{:S(2)}) async-start(), calls=%async_computation.3 | async-start | bytes 4456448 | tf_op jit(solution)/shard_map/reduce_scatter | solution.py:51
  198.8 0.8 copy-start.3
  198.8 9.6 %copy-start.5 = (f32[256,32]{0,1:T(8,128)S(1)}, f32[256,32]{0,1:T(8,128)}, u32[]{:S(2)}) copy-start(f32[256,32]{0,1:T(8,128)} %param.10) | copy-start | bytes 98308
  198.8 415.0 %all-reduce.6.cloned.1.call-start = ((), (), s32[]{:S(2)}) async-start(), calls=%async_computation.7 | async-start | bytes 132096 | tf_op jit(solution)/shard_map/psum | solution.py:79
  206.8 54.0 %copy-start.2 = (f32[64,8,256]{2,1,0:T(8,128)S(1)}, f32[64,8,256]{2,1,0:T(8,128)}, u32[]{:S(2)}) copy-start(f32[64,8,256]{2,1,0:T(8,128)} %param.8) | copy-start | bytes 1572868
  206.8 55.4 %copy-start.6 = (f32[256,32]{0,1:T(8,128)S(1)}, f32[256,32]{0,1:T(8,128)}, u32[]{:S(2)}) copy-start(f32[256,32]{0,1:T(8,128)} %param.9) | copy-start | bytes 98308
  209.0 156.1 %copy-start.7 = (f32[128]{0:T(128)S(1)}, f32[128]{0:T(128)}, u32[]{:S(2)}) copy-start(f32[128]{0:T(128)} %param.12) | copy-start | bytes 1540
  262.9 607.0 %all-reduce.4.cloned.1.call-start = ((), (), s32[]{:S(2)}) async-start(), calls=%async_computation.6 | async-start | bytes 1048576 | tf_op jit(solution)/shard_map/psum | solution.py:79
Sparse Core Ops, SparseCore 0:
  10.5 100.4 all-gather.4
  114.1 66.3 all-gather.2
  184.8 74.8 reduce-scatter.4
  262.2 99.0 reduce-scatter.2
  367.7 246.0 all-reduce.5
  619.7 250.0 all-reduce.3
where the time goes:
time: 884 us; the launch traced here: 882 us
  waiting for transfers between devices  798 us (90%)
  matrix products  39 us (4%)
  local copies, waits for them, and re-layouts  24.2 us (3%)
  between operations  14.3 us (2%)
    psum x2, waiting for transfers between devices, body(): lax.psum((grad_wleft, grad_wright, grad_out, grad_bpart), ('seq', 'res'))  503 us
    reduce_scatter x1, waiting for transfers between devices, body(): lax.psum_scatter(partial_value, 'seq', scatter_dimension=0, tiled=True)  98.3 us
    all_gather x1, waiting for transfers between devices, body(): grad_full = lax.all_gather(local_grad, 'seq', axis=0, tiled=True)  93.4 us
    all_gather x1, waiting for transfers between devices, body(): left_full = lax.all_gather(left_rows, 'res', axis=1, tiled=True)  53.7 us
    reduce_scatter x1, waiting for transfers between devices, body(): lax.psum_scatter(grad_left_part, 'res', scatter_dimension=1, tiled=True)  49.6 us
  transfers between devices with their start and end apart: 6, of which 6 were waited for; matrix products, arithmetic and copies ran while one was open for 7% of the time, Pallas kernels for 0%

commit v1 on v0

v1 whole, which is shorter than its diff:
```python
import functools

import jax
import jax.numpy as jnp
from jax import lax
from jax.experimental import pallas as pl
from jax.experimental.pallas import tpu as pltpu
from jax.sharding import PartitionSpec as P

EPS = 1e-05
F32 = jnp.float32
BF16 = jnp.bfloat16
MESH = pl.DeviceIdType.MESH
NN = (((1,), (0,)), ((), ()))
NT = (((1,), (1,)), ((), ()))


def mm(a, b, dims=NN):
    return lax.dot_general(a, b, dims, preferred_element_type=F32)


def split(x):
    high = x.astype(BF16)
    return high, (x - high.astype(F32)).astype(BF16)


def mm3(a, b, dims=NN):
    return mm(a[0], b[0], dims) + (mm(a[0], b[1], dims) + mm(a[1], b[0], dims))


def signal_peers(axes):
    barrier = pltpu.get_barrier_semaphore()
    for axis in axes:
        size = lax.axis_size(axis)
        me = lax.axis_index(axis)

        def signal(step, _, me=me, size=size, axis=axis):
            pl.semaphore_signal(
                barrier,
                inc=1,
                device_id={axis: lax.rem(me + step, size)},
                device_id_type=MESH,
            )
            return 0

        lax.fori_loop(1, size, signal, 0)


def wait_peers(axes):
    total = sum(lax.axis_size(axis) - 1 for axis in axes)
    pl.semaphore_wait(pltpu.get_barrier_semaphore(), total)


class Exchange:
    def __init__(self, axis, src_of, dst_of, send_sem, recv_sem):
        self.axis = axis
        self.size = lax.axis_size(axis)
        self.me = lax.axis_index(axis)
        self.src_of = src_of
        self.dst_of = dst_of
        self.send_sem = send_sem
        self.recv_sem = recv_sem

    def copy(self, target, slot):
        return pltpu.make_async_remote_copy(
            src_ref=self.src_of(target),
            dst_ref=self.dst_of(slot),
            send_sem=self.send_sem.at[target],
            recv_sem=self.recv_sem.at[slot],
            device_id={self.axis: target},
            device_id_type=MESH,
        )

    def each(self, act):
        def one(step, _):
            act(lax.rem(self.me + step, self.size))
            return 0

        lax.fori_loop(1, self.size, one, 0)

    def start(self):
        self.each(lambda peer: self.copy(peer, self.me).start())

    def wait_recv(self):
        self.each(lambda peer: self.copy(peer, peer).wait_recv())

    def wait_send(self):
        self.each(lambda peer: self.copy(peer, self.me).wait_send())


def block(index, rows):
    return pl.ds(pl.multiple_of(index * rows, rows), rows)


def norm_rows(x_ref, normed, inverse, own, depth):
    def one(i, _):
        x = jnp.concatenate(
            [x_ref[pl.ds(i + p * own, depth, stride=2 * own), :] for p in range(2)], axis=1
        )
        centred = x - jnp.mean(x, axis=-1, keepdims=True)
        inv = lax.rsqrt(jnp.mean(centred * centred, axis=-1, keepdims=True) + EPS)
        normed[block(i, depth), :] = centred * inv
        inverse[block(i, depth), :] = inv
        return 0

    lax.fori_loop(0, own, one, 0)


def norm_back(upstream, normed, inverse, out_ref, own, depth):
    for i in range(own):
        rows = slice(i * depth, (i + 1) * depth)
        u = upstream[rows, :]
        y = normed[rows, :]
        first = jnp.mean(u, axis=-1, keepdims=True)
        second = jnp.mean(u * y, axis=-1, keepdims=True)
        g = inverse[rows, :] * (u - first - y * second)
        for p in range(2):
            lanes = slice(p * 128, (p + 1) * 128)
            out_ref[pl.ds(i + p * own, depth, stride=2 * own), :] = g[:, lanes]


def kernel(
    src, tgt, wl_t, wr_t, fin, bias, cot,
    edge_out, cols_out, rows_out, fin_out, gl_out, gr_out, gb_out,
    xs, xs_inv, xt, xt_inv, turn, left_blk, left_all, left_h, left_l, lt_h, lt_l,
    cot_blk, cot_all, cot_h, cot_l, fin_h, fin_l, b_h, b_l,
    gls_part, gls_in, edge_part, edge_in, db_h, db_l, acc64, acc32, grs_ref, up,
    big, big_in, small, small_in, acc1, in2, acc2, seqs, red,
    s_cot, r_cot, s_left, r_left, s_gls, r_gls, s_edge, r_edge,
    s_big, r_big, s_small, r_small, s_p2, r_p2, s_p3, r_p3, s_p4, r_p4,
    *, own, depth, hid, wide,
):
    nr = lax.axis_size("res")
    ns = lax.axis_size("seq")
    res_me = lax.axis_index("res")
    seq_me = lax.axis_index("seq")
    scale = 1.0 / (depth * ns)
    pairs = hid // 2
    half = depth
    tile = 2 * depth
    full = own * nr
    signal_peers(("seq", "res"))

    norm_rows(src, xs, xs_inv, own, depth)
    wl_ts = split(wl_t[...])
    left_t = mm3(wl_ts, split(xs[...]), NT)
    low = lax.broadcasted_iota(jnp.int32, (hid, tile), 1) < half
    for u in range(own // 2):
        a = left_t[:, u * tile : (u + 1) * tile]
        b = pltpu.roll(a, half, 1)
        turn[2 * u * hid : (2 * u + 1) * hid, :] = jnp.where(low, a, b)
        turn[(2 * u + 1) * hid : (2 * u + 2) * hid, :] = jnp.where(low, b, a)
    low8 = lax.broadcasted_iota(jnp.int32, (own, tile), 1) < half
    for t in range(pairs):
        even = turn[pl.ds(2 * t, own, stride=hid), :]
        odd = turn[pl.ds(2 * t + 1, own, stride=hid), :]
        left_blk[:, t * tile : (t + 1) * tile] = jnp.where(low8, even, odd)
    for j in range(own):
        cot_blk[:, j * wide : (j + 1) * wide] = cot[pl.ds(j, own, stride=own), :]

    wait_peers(("seq", "res"))
    x_cot = Exchange("seq", lambda t: cot_blk, lambda k: cot_all.at[block(k, own)], s_cot, r_cot)
    x_left = Exchange("res", lambda t: left_blk, lambda k: left_all.at[block(k, own)], s_left, r_left)
    x_cot.start()
    x_left.start()
    cot_all[block(seq_me, own), :] = cot_blk[...]
    left_all[block(res_me, own), :] = left_blk[...]

    norm_rows(tgt, xt, xt_inv, own, depth)
    wr_ts = split(wr_t[...])
    right = mm3(split(xt[...]), wr_ts, NT) * scale
    right_h, right_l = split(right)
    right_k = jnp.concatenate([right_h, right_h, right_l], axis=1)
    rt_h, rt_l = split(right.T)
    rt_hl = jnp.concatenate([rt_h, rt_l], axis=0)
    fh, fl = split(fin[...])
    fin_h[...] = fh
    fin_l[...] = fl

    def make_b(hp, _):
        def stacked(p):
            rows = block(2 * hp + p, hid)
            return jnp.concatenate([fin_h[rows, :], fin_l[rows, :], fin_h[rows, :]], axis=0)

        val = mm(right_k, jnp.concatenate([stacked(0), stacked(1)], axis=1))
        for p in range(2):
            for j in range(own):
                v = val[j * depth : (j + 1) * depth, p * wide : (p + 1) * wide]
                vh, vl = split(v)
                b_h[block(2 * hp + p, depth), j * wide : (j + 1) * wide] = vh
                b_l[block(2 * hp + p, depth), j * wide : (j + 1) * wide] = vl
        return 0

    lax.fori_loop(0, pairs, make_b, 0)

    x_cot.wait_recv()
    ch, cl = split(cot_all[...])
    cot_h[...] = ch
    cot_l[...] = cl

    def make_gls(n, _):
        rows = block(n, 2 * tile)
        gls_part[:, block(n, 2 * tile)] = mm3(
            (cot_h[...], cot_l[...]), (b_h[rows, :], b_l[rows, :]), NT
        )
        return 0

    lax.fori_loop(0, hid * depth // (2 * tile), make_gls, 0)
    x_gls = Exchange("res", lambda t: gls_part.at[block(t, own)], lambda k: gls_in.at[k], s_gls, r_gls)
    x_gls.start()
    gls_in[res_me] = gls_part[block(res_me, own), :]

    x_left.wait_recv()
    lh, ll = split(left_all[...])
    left_h[...] = lh
    left_l[...] = ll
    for t in range(pairs):
        th, tl = split(left_all[:, t * tile : (t + 1) * tile].T)
        lt_h[t * tile : (t + 1) * tile, :] = th
        lt_l[t * tile : (t + 1) * tile, :] = tl
    acc64[...] = jnp.zeros_like(acc64)
    acc32[...] = jnp.zeros_like(acc32)

    def make_db(hp, _):
        a_h = lt_h[block(hp, tile), :]
        a_l = lt_l[block(hp, tile), :]
        a_hl = jnp.concatenate([a_h, a_l], axis=1)
        for jj in range(own // 2):
            cols = slice(2 * jj * wide, 2 * (jj + 1) * wide)
            c_h = cot_h[:, cols]
            val = mm(a_hl, jnp.concatenate([c_h, c_h], axis=0)) + mm(a_h, cot_l[:, cols])
            for q in range(2):
                for p in range(2):
                    v = val[p * depth : (p + 1) * depth, q * wide : (q + 1) * wide]
                    vh, vl = split(v)
                    rows = slice((2 * jj + q) * depth, (2 * jj + q + 1) * depth)
                    db_h[rows, p * wide : (p + 1) * wide] = vh
                    db_l[rows, p * wide : (p + 1) * wide] = vl
        dh = db_h[...]
        dl = db_l[...]
        y = mm(rt_hl, dh)
        grad = y[:hid, :] + y[hid:, :] + mm(rt_h, dl)
        quad = hp // 2
        lanes = pl.ds(pl.multiple_of((hp % 2) * 2 * wide, 2 * wide), 2 * wide)
        big[:, quad, :, lanes] = grad.reshape(hid, 1, 2 * wide)

        def flat(ref):
            return jnp.concatenate(
                [ref[block(2 * hp, hid), :], ref[block(2 * hp + 1, hid), :]], axis=1
            )

        f_h = flat(fin_h)
        acc64[...] += mm(dh, jnp.concatenate([f_h, flat(fin_l)], axis=0), NT)
        acc32[...] += mm(dl, f_h, NT)
        return 0

    lax.fori_loop(0, pairs, make_db, 0)
    per = hid // nr
    x_big = Exchange("res", lambda t: big.at[pl.ds(t * per, per)], lambda k: big_in.at[k], s_big, r_big)
    x_big.start()
    big_in[res_me] = big[pl.ds(res_me * per, per)]

    def make_edge(n, _):
        cols = block(n, 2 * wide)
        edge_part[:, cols] = mm3((left_h[...], left_l[...]), (b_h[:, cols], b_l[:, cols]))
        return 0

    lax.fori_loop(0, own * wide // (2 * wide), make_edge, 0)
    x_edge = Exchange("seq", lambda t: edge_part.at[block(t, own)], lambda k: edge_in.at[k], s_edge, r_edge)
    x_edge.start()
    edge_in[seq_me] = edge_part[block(seq_me, own), :]

    both = acc64[...]
    grs = (both[:, :hid] + both[:, hid:] + acc32[...]) * scale
    xts = split(xt[...])
    up[...] = mm3(split(grs), wr_ts)
    norm_back(up, xt, xt_inv, cols_out, own, depth)
    gr_t = mm3(split(grs.T), xts)
    gb = jnp.sum(cot[...], axis=0, keepdims=True)
    for h in range(2):
        small[:, 2 + h, :, :] = gr_t[:, h * wide : (h + 1) * wide].reshape(hid, 1, wide)
    small[:, 4, :, :] = jnp.broadcast_to(gb, (hid, wide)).reshape(hid, 1, wide)
    for h in range(5, 8):
        small[:, h, :, :] = jnp.zeros((hid, 1, wide), F32)

    x_gls.wait_recv()
    gls = gls_in[0]
    for k in range(1, nr):
        gls = gls + gls_in[k]
    for t in range(pairs):
        v = gls[:, t * tile : (t + 1) * tile]
        turn[pl.ds(2 * t, own, stride=hid), :] = v
        turn[pl.ds(2 * t + 1, own, stride=hid), :] = pltpu.roll(v, half, 1)
    parts = []
    for u in range(own // 2):
        a = turn[2 * u * hid : (2 * u + 1) * hid, :]
        b = turn[(2 * u + 1) * hid : (2 * u + 2) * hid, :]
        parts.append(jnp.where(low, a, pltpu.roll(b, half, 1)))
    gls_t = jnp.concatenate(parts, axis=1)
    gl_t = mm3(split(gls_t), split(xs[...]))
    for h in range(2):
        small[:, h, :, :] = gl_t[:, h * wide : (h + 1) * wide].reshape(hid, 1, wide)
    x_small = Exchange("res", lambda t: small.at[pl.ds(t * per, per)], lambda k: small_in.at[k], s_small, r_small)
    x_small.start()
    small_in[res_me] = small[pl.ds(res_me * per, per)]
    up[...] = mm3(split(gls_t.T), wl_ts)
    norm_back(up, xs, xs_inv, rows_out, own, depth)

    x_big.wait_recv()
    x_small.wait_recv()
    acc1[:, :, :, : 4 * wide] = jnp.sum(big_in[...], axis=0)
    acc1[:, :, :, 4 * wide :] = jnp.sum(small_in[...], axis=0)
    few, quads = seq_chunk(per, ns)
    groups = 8 // quads

    def at(ref, t):
        return ref.at[pl.ds((t // groups) * few, few), pl.ds((t % groups) * quads, quads)]

    x_p2 = Exchange("seq", lambda t: at(acc1, t), lambda k: in2.at[k], s_p2, r_p2)
    x_p2.start()
    in2[seq_me] = at(acc1, seq_me)[...]
    x_p2.wait_recv()
    acc2[...] = jnp.sum(in2[...], axis=0)
    x_p3 = Exchange("seq", lambda t: acc2, lambda k: at(seqs, k), s_p3, r_p3)
    x_p3.start()
    at(seqs, seq_me)[...] = acc2[...]
    x_p3.wait_recv()
    x_p4 = Exchange("res", lambda t: seqs, lambda k: red.at[pl.ds(k * per, per)], s_p4, r_p4)
    x_p4.start()
    red[pl.ds(res_me * per, per)] = seqs[...]

    x_edge.wait_recv()
    edge = edge_in[0]
    for k in range(1, ns):
        edge = edge + edge_in[k]
    for j in range(own):
        edge_out[pl.ds(j, own, stride=own), :] = edge[:, j * wide : (j + 1) * wide] + bias[...]

    x_p4.wait_recv()
    for h in range(hid):
        fin_out[h * hid : (h + 1) * hid, :] = red[:, h // 4, :, (h % 4) * wide : (h % 4 + 1) * wide].reshape(hid, wide)
    for h in range(2):
        lanes = slice(h * wide, (h + 1) * wide)
        gl_out[:, lanes] = red[:, h, :, 4 * wide :].reshape(hid, wide)
        gr_out[:, lanes] = red[:, 2 + h, :, 4 * wide :].reshape(hid, wide)
    gb_out[...] = red[0, 4, :, 4 * wide :]
    for x in (x_cot, x_left, x_gls, x_edge, x_big, x_small, x_p2, x_p3, x_p4):
        x.wait_send()


def seq_chunk(per, ns):
    quads = max(1, 8 // ns)
    return per * 8 // (ns * quads), quads


def to_tiles(x):
    depth, own, chan = x.shape
    return x.reshape(depth, own, 2, chan // 2).swapaxes(1, 2).reshape(-1, chan // 2)


def from_tiles(x, depth, own):
    return x.reshape(depth, 2, own, -1).swapaxes(1, 2).reshape(depth, own, -1)


def body(tgt, src, wl, wr, fin, bias, cot):
    ns = lax.axis_size("seq")
    nr = lax.axis_size("res")
    depth, own, chan = src.shape
    hid = wl.shape[1]
    wide = fin.shape[1]
    flat = own * depth
    per = hid // nr
    few, quads = seq_chunk(per, ns)
    v = pltpu.VMEM
    k = hid * depth
    n = own * wide
    operands = (
        to_tiles(src), to_tiles(tgt), wl.T, wr.T, fin,
        bias.reshape(1, wide), cot.reshape(own * own, wide),
    )
    outs = (
        jax.ShapeDtypeStruct((own * own, wide), F32),
        jax.ShapeDtypeStruct((2 * flat, 128), F32),
        jax.ShapeDtypeStruct((2 * flat, 128), F32),
        jax.ShapeDtypeStruct((hid * hid, wide), F32),
        jax.ShapeDtypeStruct((hid, chan), F32),
        jax.ShapeDtypeStruct((hid, chan), F32),
        jax.ShapeDtypeStruct((1, wide), F32),
    )
    scratch = [
        v((flat, chan), F32), v((flat, 1), F32), v((flat, chan), F32), v((flat, 1), F32),
        v((own * hid, 2 * depth), F32), v((own, k), F32), v((nr * own, k), F32),
        v((nr * own, k), BF16), v((nr * own, k), BF16), v((k, nr * own), BF16), v((k, nr * own), BF16),
        v((own, n), F32), v((ns * own, n), F32), v((ns * own, n), BF16), v((ns * own, n), BF16),
        v((hid * hid, wide), BF16), v((hid * hid, wide), BF16), v((k, n), BF16), v((k, n), BF16),
        v((nr * own, k), F32), v((nr, own, k), F32), v((ns * own, n), F32), v((ns, own, n), F32),
        v((flat, 2 * wide), BF16), v((flat, 2 * wide), BF16), v((flat, 2 * hid), F32), v((flat, hid), F32),
        v((flat, hid), F32), v((flat, chan), F32),
        v((hid, 8, 1, 4 * wide), F32), v((nr, per, 8, 1, 4 * wide), F32),
        v((hid, 8, 1, wide), F32), v((nr, per, 8, 1, wide), F32),
        v((per, 8, 1, 5 * wide), F32), v((ns, few, quads, 1, 5 * wide), F32), v((few, quads, 1, 5 * wide), F32),
        v((per, 8, 1, 5 * wide), F32), v((hid, 8, 1, 5 * wide), F32),
    ]
    for axis in (ns, ns, nr, nr, nr, nr, ns, ns, nr, nr, nr, nr, ns, ns, ns, ns, nr, nr):
        scratch.append(pltpu.SemaphoreType.DMA((axis,)))
    spec = pl.BlockSpec(memory_space=pltpu.MemorySpace.VMEM)
    edge, cols, rows, g_fin, g_wl, g_wr, g_bias = pl.pallas_call(
        functools.partial(kernel, own=own, depth=depth, hid=hid, wide=wide),
        out_shape=outs,
        in_specs=[spec] * len(operands),
        out_specs=(spec,) * len(outs),
        scratch_shapes=scratch,
        compiler_params=pltpu.CompilerParams(
            collective_id=0, has_side_effects=True, vmem_limit_bytes=60 * 2**20
        ),
        name="outer_mean",
    )(*operands)
    return (
        edge.reshape(own, own, wide),
        from_tiles(cols, depth, own),
        from_tiles(rows, depth, own),
        g_wl.T,
        g_wr.T,
        g_fin,
        g_bias.reshape(wide),
    )


def solution(mesh):
    parts = P("seq", "res", None)
    in_specs = (parts, parts, P(), P(), P(), P(), parts)
    out_specs = (parts, parts, parts, P(), P(), P(), P())
    return jax.shard_map(body, mesh=mesh, in_specs=in_specs, out_specs=out_specs, check_vma=False)
```

time: 884 us -> 93.4 us (0.11)
  waiting for transfers between devices: 798 us -> 0 us
  Pallas kernels: 0 us -> 85.7 us
  matrix products: 39 us -> 0 us
  local copies, waits for them, and re-layouts: 24.2 us -> 6.8 us
  between operations: 14.3 us -> 0.65 us
    psum x2 -> x0, waiting for transfers between devices: 503 us -> none  [body(): lax.psum((grad_wleft, grad_wright, grad_out, grad_bpart), ('seq', 'res'))]
    reduce_scatter x2 -> x0, waiting for transfers between devices: 148 us -> none  [the longest x1 98.3 us: body(): lax.psum_scatter(partial_value, 'seq', scatter_dimension=0, tiled=True)]
    all_gather x2 -> x0, waiting for transfers between devices: 147 us -> none  [the longest x1 93.4 us: body(): grad_full = lax.all_gather(local_grad, 'seq', axis=0, tiled=True)]
    pallas_call x0 -> x1, Pallas kernels: none -> 85.7 us  [body(): pl.pallas_call(functools.partial(kernel, own=own, depth=depth, hid=hid, w...]
    dot_general x12 -> x0, matrix products: 39 us -> none  [the longest x1 10.2 us: body(): jnp.einsum('ijhk,sjk->sih', grad_four, right_cols, precision=exact_arithm...]
    all_gather x2 -> x0, local copies, waits for them, and re-layouts: 9.79 us -> none  [the longest x1 5.42 us: body(): grad_full = lax.all_gather(local_grad, 'seq', axis=0, tiled=True)]
  transfers between devices with their start and end apart: 6 -> 0, of which waited for: 6 -> 0; matrix products, arithmetic and copies ran while one was open for 7% -> 0% of each run, Pallas kernels for 0% -> 0%
where the time goes in v1:
time: 93.4 us; the launch traced here: 93.2 us
  Pallas kernels  85.7 us (92%)
  local copies, waits for them, and re-layouts  6.8 us (7%)
    pallas_call x1, Pallas kernels, body(): pl.pallas_call(functools.partial(kernel, own=own, depth=depth, hid=hid, w...  85.7 us
    unnamed x17, local copies, waits for them, and re-layouts  6.8 us

profile of v1, /device:TPU:1, one launch (start us, length us, event | category | flops | bytes accessed | tf_op | source)
XLA Modules:
  0.0 93.2 jit_solution(8747716148073811738)
XLA Ops:
  0.6 85.7 %outer_mean.1 = (f32[64,128]{1,0:T(8,128)}, f32[1024,128]{1,0:T(8,128)}, f32[1024,128]{1,0:T(8,128)}, f32[1024,128]{1,0:T(8,128)}, f32[32,256]{1,0:T(8,128)}, /*index=5*/f32[32,256]{1,0:T(8,128)}, f32[1,128]{1,0:T(1,128)}) custom-call(f32[1024,128]{1,0:T(8,128)} %bitcast.28, f32[1024,128]{1,0:T(8,128)} %bitcast.29, f32[32,256]{1,0:T(8,128)} %bitcast.32, ...), custom_call_target="tpu_custom_call" | custom-call | tf_op jit(solution)/shard_map/outer_mean/pallas_call | solution.py:407
  86.4 1.4 %copy.21 = f32[8,8,128]{2,1,0:T(8,128)} copy(f32[8,8,128]{2,1,0:T(8,128)} %bitcast.37) | data formatting | bytes 65536
  87.7 0.0 copy-start.1
  87.7 1.9 %copy.22 = f32[64,8,256]{2,1,0:T(8,128)} copy(f32[64,8,256]{2,1,0:T(8,128)} %bitcast.31) | data formatting | bytes 1048576
  89.7 0.0 copy-done.1
  89.7 0.0 copy-start.3
  89.7 0.0 copy-start
  89.7 0.8 copy.23
  90.5 0.0 copy-done.3
  90.5 0.0 copy-start.2
  90.5 0.6 copy.24
  91.1 0.2 copy-done.2
  91.2 0.6 copy.25
  91.9 0.0 copy-done
  91.9 0.0 copy-start.4
  91.9 0.8 copy.26
  92.7 0.0 copy-done.4
  92.7 0.5 copy.27
Async XLA Ops:
  87.7 1.9 %copy-start.1 = (f32[1024,128]{1,0:T(8,128)S(1)}, f32[1024,128]{1,0:T(8,128)}, u32[]{:S(2)}) copy-start(f32[1024,128]{1,0:T(8,128)} %get-tuple-element.16) | copy-start | bytes 1572868
  89.7 0.8 copy-start.3
  89.7 2.2 %copy-start = (f32[1024,128]{1,0:T(8,128)S(1)}, f32[1024,128]{1,0:T(8,128)}, u32[]{:S(2)}) copy-start(f32[1024,128]{1,0:T(8,128)} %get-tuple-element.33) | copy-start | bytes 1572868
  90.5 0.8 copy-start.2
  91.9 0.8 copy-start.4

commit v2 on v1

--- a/solution.py
+++ b/solution.py
@@ -8,6 +8,8 @@
 from jax.sharding import PartitionSpec as P
 
 EPS = 1e-05
+RES = (2, 4, 2)
+SEMS = 192
 F32 = jnp.float32
 BF16 = jnp.bfloat16
 MESH = pl.DeviceIdType.MESH
@@ -28,64 +30,81 @@
     return mm(a[0], b[0], dims) + (mm(a[0], b[1], dims) + mm(a[1], b[0], dims))
 
 
-def signal_peers(axes):
-    barrier = pltpu.get_barrier_semaphore()
-    for axis in axes:
-        size = lax.axis_size(axis)
-        me = lax.axis_index(axis)
-
-        def signal(step, _, me=me, size=size, axis=axis):
-            pl.semaphore_signal(
-                barrier,
-                inc=1,
-                device_id={axis: lax.rem(me + step, size)},
-                device_id_type=MESH,
-            )
+class Group:
+    def __init__(self, size, me, id_of):
+        self.size = size
+        self.me = me
+        self.id_of = id_of
+
+    def each(self, act):
+        def one(step, _):
+            act(lax.rem(self.me + step, self.size))
             return 0
 
-        lax.fori_loop(1, size, signal, 0)
-
-
-def wait_peers(axes):
-    total = sum(lax.axis_size(axis) - 1 for axis in axes)
-    pl.semaphore_wait(pltpu.get_barrier_semaphore(), total)
+        if self.size > 1:
+            lax.fori_loop(1, self.size, one, 0)
+
+
+class Semaphores:
+    def __init__(self, send, recv):
+        self.send = send
+        self.recv = recv
+        self.used = 0
+
+    def take(self, count):
+        self.used += count
+        return self.used - count
 
 
 class Exchange:
-    def __init__(self, axis, src_of, dst_of, send_sem, recv_sem):
-        self.axis = axis
-        self.size = lax.axis_size(axis)
-        self.me = lax.axis_index(axis)
+    def __init__(self, group, sems, src_of, dst_of):
+        self.group = group
+        self.sems = sems
+        self.base = sems.take(group.size)
         self.src_of = src_of
         self.dst_of = dst_of
-        self.send_sem = send_sem
-        self.recv_sem = recv_sem
 
     def copy(self, target, slot):
         return pltpu.make_async_remote_copy(
             src_ref=self.src_of(target),
             dst_ref=self.dst_of(slot),
-            send_sem=self.send_sem.at[target],
-            recv_sem=self.recv_sem.at[slot],
-            device_id={self.axis: target},
+            send_sem=self.sems.send.at[self.base + target],
+            recv_sem=self.sems.recv.at[self.base + slot],
+            device_id=self.group.id_of(target),
             device_id_type=MESH,
         )
 
-    def each(self, act):
-        def one(step, _):
-            act(lax.rem(self.me + step, self.size))
-            return 0
-
-        lax.fori_loop(1, self.size, one, 0)
+    def start_to(self, peer):
+        self.copy(peer, self.group.me).start()
+
+    def wait_from(self, peer):
+        self.copy(peer, peer).wait_recv()
 
     def start(self):
-        self.each(lambda peer: self.copy(peer, self.me).start())
+        self.group.each(self.start_to)
 
     def wait_recv(self):
-        self.each(lambda peer: self.copy(peer, peer).wait_recv())
+        self.group.each(self.wait_from)
 
     def wait_send(self):
-        self.each(lambda peer: self.copy(peer, self.me).wait_send())
+        self.group.each(lambda peer: self.copy(peer, self.group.me).wait_send())
+
+
+def signal_peers(groups):
+    barrier = pltpu.get_barrier_semaphore()
+    for group in groups:
+
+        def signal(peer, group=group):
+            pl.semaphore_signal(
+                barrier, inc=1, device_id=group.id_of(peer), device_id_type=MESH
+            )
+
+        group.each(signal)
+
+
+def wait_peers(groups):
+    total = sum(group.size - 1 for group in groups)
+    pl.semaphore_wait(pltpu.get_barrier_semaphore(), total)
 
 
 def block(index, rows):
@@ -124,10 +143,10 @@
     edge_out, cols_out, rows_out, fin_out, gl_out, gr_out, gb_out,
     xs, xs_inv, xt, xt_inv, turn, left_blk, left_all, left_h, left_l, lt_h, lt_l,
     cot_blk, cot_all, cot_h, cot_l, fin_h, fin_l, b_h, b_l,
-    gls_part, gls_in, edge_part, edge_in, db_h, db_l, acc64, acc32, grs_ref, up,
-    big, big_in, small, small_in, acc1, in2, acc2, seqs, red,
-    s_cot, r_cot, s_left, r_left, s_gls, r_gls, s_edge, r_edge,
-    s_big, r_big, s_small, r_small, s_p2, r_p2, s_p3, r_p3, s_p4, r_p4,
+    gls_part, gls_c, gls_1, gls_x, gls_2, gls_y,
+    edge_part, edge_in, db_h, db_l, acc64, acc32, grs_ref, up,
+    big, big_c, big_1, big_x, small, small_c, small_1, small_x,
+    acc1, in2, acc2, seqs, red, send_sem, recv_sem,
     *, own, depth, hid, wide,
 ):
     nr = lax.axis_size("res")
@@ -139,7 +158,25 @@
     half = depth
     tile = 2 * depth
     full = own * nr
-    signal_peers(("seq", "res"))
+    yn, xn, cn = RES
+    core = lax.rem(res_me, cn)
+    ex = lax.rem(res_me // cn, xn)
+    wy = res_me // (cn * xn)
+    others = [lax.rem(wy + d, yn) for d in range(1, yn)]
+
+    def res_id(y, x, c):
+        return (y * xn + x) * cn + c
+
+    g_core = Group(cn, core, lambda m: {"res": res_id(wy, ex, m)})
+    g_x = Group(xn, ex, lambda m: {"res": res_id(wy, m, core)})
+    g_y = Group(yn, wy, lambda m: {"res": res_id(m, ex, core)})
+    g_seq = Group(ns, seq_me, lambda m: {"seq": m})
+    g_far = Group(
+        yn * ns, wy * ns + seq_me, lambda m: {"res": res_id(m // ns, ex, core), "seq": lax.rem(m, ns)}
+    )
+    greeted = (g_core, g_x, g_far)
+    sems = Semaphores(send_sem, recv_sem)
+    signal_peers(greeted)
 
     norm_rows(src, xs, xs_inv, own, depth)
     wl_ts = split(wl_t[...])
@@ -158,15 +195,41 @@
     for j in range(own):
         cot_blk[:, j * wide : (j + 1) * wide] = cot[pl.ds(j, own, stride=own), :]
 
-    wait_peers(("seq", "res"))
-    x_cot = Exchange("seq", lambda t: cot_blk, lambda k: cot_all.at[block(k, own)], s_cot, r_cot)
-    x_left = Exchange("res", lambda t: left_blk, lambda k: left_all.at[block(k, own)], s_left, r_left)
+    wait_peers(greeted)
+
+    def left_at(y, x, c):
+        return left_all.at[block(res_id(y, x, c), own)]
+
+    x_cot = Exchange(g_seq, sems, lambda t: cot_blk, lambda k: cot_all.at[block(k, own)])
+    left_xs = Exchange(g_x, sems, lambda t: left_blk, lambda k: left_at(wy, k, core))
+    left_ys = Exchange(g_y, sems, lambda t: left_blk, lambda k: left_at(k, ex, core))
+    left_far = [
+        Exchange(g_x, sems, lambda t, y=y: left_at(y, ex, core), lambda k, y=y: left_at(y, k, core))
+        for y in others
+    ]
+    left_own = Exchange(g_core, sems, lambda t: left_blk, lambda k: left_at(wy, ex, k))
+
+    def to_core(y, x):
+        return Exchange(
+            g_core, sems, lambda t: left_at(y, x, core), lambda k: left_at(y, x, k)
+        )
+
+    left_mates = [to_core(y, ex) for y in others]
+    steps = [lax.rem(ex + d, xn) for d in range(1, xn)]
+    left_mates_x = [to_core(wy, x) for x in steps]
+    left_mates_far = [[to_core(y, x) for x in steps] for y in others]
+    left_ys.start()
+    left_xs.start()
+    left_own.start()
     x_cot.start()
-    x_left.start()
     cot_all[block(seq_me, own), :] = cot_blk[...]
     left_all[block(res_me, own), :] = left_blk[...]
 
     norm_rows(tgt, xt, xt_inv, own, depth)
+    left_ys.wait_recv()
+    for far, mate in zip(left_far, left_mates):
+        far.start()
+        mate.start()
     wr_ts = split(wr_t[...])
     right = mm3(split(xt[...]), wr_ts, NT) * scale
     right_h, right_l = split(right)
@@ -206,11 +269,45 @@
         return 0
 
     lax.fori_loop(0, hid * depth // (2 * tile), make_gls, 0)
-    x_gls = Exchange("res", lambda t: gls_part.at[block(t, own)], lambda k: gls_in.at[k], s_gls, r_gls)
-    x_gls.start()
-    gls_in[res_me] = gls_part[block(res_me, own), :]
-
-    x_left.wait_recv()
+    def gls_at(y, x, c):
+        return gls_part.at[block(res_id(y, x, c), own)]
+
+    mate_gls = {}
+    for y in range(yn):
+        for x in range(xn):
+            mate_gls[y, x] = Exchange(
+                g_core,
+                sems,
+                lambda t, y=y, x=x: gls_at(y, x, t),
+                lambda k, y=y, x=x: gls_c.at[y * xn + x],
+            )
+            mate_gls[y, x].start()
+    for x, mate in zip(steps, left_mates_x):
+        left_xs.wait_from(x)
+        mate.start()
+    for far, mates in zip(left_far, left_mates_far):
+        for x, mate in zip(steps, mates):
+            far.wait_from(x)
+            mate.start()
+
+    x_gls = [
+        Exchange(
+            g_x, sems, lambda t, y=y: gls_1.at[y * xn + t], lambda k, y=y: gls_x.at[y * xn + k]
+        )
+        for y in [wy, *others]
+    ]
+    for (y, x), mate in mate_gls.items():
+        mate.wait_recv()
+        at = y * xn + x
+        if cn > 1:
+            gls_1[at] = gls_at(y, x, core)[...] + gls_c[at]
+        else:
+            gls_1[at] = gls_at(y, x, core)[...]
+    for sent in reversed(x_gls):
+        sent.start()
+
+    for mate in [left_own, *left_mates, *left_mates_x, *sum(left_mates_far, [])]:
+        mate.wait_recv()
     lh, ll = split(left_all[...])
     left_h[...] = lh
     left_l[...] = ll
@@ -255,10 +352,28 @@
         return 0
 
     lax.fori_loop(0, pairs, make_db, 0)
-    per = hid // nr
-    x_big = Exchange("res", lambda t: big.at[pl.ds(t * per, per)], lambda k: big_in.at[k], s_big, r_big)
-    x_big.start()
-    big_in[res_me] = big[pl.ds(res_me * per, per)]
+    per_c = hid // cn
+    per = per_c // xn
+
+    def start_core(whole, mine):
+        out = Exchange(g_core, sems, lambda t: whole.at[pl.ds(t * per_c, per_c)], lambda k: mine)
+        out.start()
+        return out
+
+    def fold_core(exchange, whole, other, total):
+        exchange.wait_recv()
+        if cn > 1:
+            total[...] = whole[pl.ds(core * per_c, per_c)] + other[...]
+        else:
+            total[...] = whole[...]
+
+    def start_x(total, arrived):
+        out = Exchange(g_x, sems, lambda t: total.at[pl.ds(t * per, per)], lambda k: arrived.at[k])
+        out.start()
+        arrived[ex] = total[pl.ds(ex * per, per)]
+        return out
+
+    core_big = start_core(big, big_c)
 
     def make_edge(n, _):
         cols = block(n, 2 * wide)
@@ -266,7 +381,11 @@
         return 0
 
     lax.fori_loop(0, own * wide // (2 * wide), make_edge, 0)
-    x_edge = Exchange("seq", lambda t: edge_part.at[block(t, own)], lambda k: edge_in.at[k], s_edge, r_edge)
+    fold_core(core_big, big, big_c, big_1)
+    x_big = start_x(big_1, big_x)
+    x_edge = Exchange(
+        g_seq, sems, lambda t: edge_part.at[block(t, own)], lambda k: edge_in.at[k]
+    )
     x_edge.start()
     edge_in[seq_me] = edge_part[block(seq_me, own), :]
 
@@ -283,10 +402,21 @@
     for h in range(5, 8):
         small[:, h, :, :] = jnp.zeros((hid, 1, wide), F32)
 
-    x_gls.wait_recv()
-    gls = gls_in[0]
-    for k in range(1, nr):
-        gls = gls + gls_in[k]
+    def fold_x(y, arriving):
+        arriving.wait_recv()
+        total = gls_1[y * xn + ex]
+        for x in steps:
+            total = total + gls_x[y * xn + x]
+        return total
+
+    y_gls = Exchange(g_y, sems, lambda t: gls_2.at[t], lambda k: gls_y.at[k])
+    for y, arriving in zip(others, x_gls[1:]):
+        gls_2[y] = fold_x(y, arriving)
+        y_gls.start_to(y)
+    gls = fold_x(wy, x_gls[0])
+    for y in others:
+        y_gls.wait_from(y)
+        gls = gls + gls_y[y]
     for t in range(pairs):
         v = gls[:, t * tile : (t + 1) * tile]
         turn[pl.ds(2 * t, own, stride=hid), :] = v
@@ -300,34 +430,47 @@
     gl_t = mm3(split(gls_t), split(xs[...]))
     for h in range(2):
         small[:, h, :, :] = gl_t[:, h * wide : (h + 1) * wide].reshape(hid, 1, wide)
-    x_small = Exchange("res", lambda t: small.at[pl.ds(t * per, per)], lambda k: small_in.at[k], s_small, r_small)
-    x_small.start()
-    small_in[res_me] = small[pl.ds(res_me * per, per)]
+    core_small = start_core(small, small_c)
     up[...] = mm3(split(gls_t.T), wl_ts)
     norm_back(up, xs, xs_inv, rows_out, own, depth)
 
+    fold_core(core_small, small, small_c, small_1)
+    x_small = start_x(small_1, small_x)
     x_big.wait_recv()
     x_small.wait_recv()
-    acc1[:, :, :, : 4 * wide] = jnp.sum(big_in[...], axis=0)
-    acc1[:, :, :, 4 * wide :] = jnp.sum(small_in[...], axis=0)
-    few, quads = seq_chunk(per, ns)
+    acc1[:, :, :, : 4 * wide] = jnp.sum(big_x[...], axis=0)
+    acc1[:, :, :, 4 * wide :] = jnp.sum(small_x[...], axis=0)
+    few, quads = far_chunk(per, g_far.size)
     groups = 8 // quads
 
     def at(ref, t):
-        return ref.at[pl.ds((t // groups) * few, few), pl.ds((t % groups) * quads, quads)]
-
-    x_p2 = Exchange("seq", lambda t: at(acc1, t), lambda k: in2.at[k], s_p2, r_p2)
+        return ref.at[pl.ds((t // groups) * few, few), pl.ds(lax.rem(t, groups) * quads, quads)]
+
+    x_p2 = Exchange(g_far, sems, lambda t: at(acc1, t), lambda k: in2.at[k])
     x_p2.start()
-    in2[seq_me] = at(acc1, seq_me)[...]
+    in2[g_far.me] = at(acc1, g_far.me)[...]
     x_p2.wait_recv()
     acc2[...] = jnp.sum(in2[...], axis=0)
-    x_p3 = Exchange("seq", lambda t: acc2, lambda k: at(seqs, k), s_p3, r_p3)
+    x_p3 = Exchange(g_far, sems, lambda t: acc2, lambda k: at(seqs, k))
     x_p3.start()
-    at(seqs, seq_me)[...] = acc2[...]
+    at(seqs, g_far.me)[...] = acc2[...]
     x_p3.wait_recv()
-    x_p4 = Exchange("res", lambda t: seqs, lambda k: red.at[pl.ds(k * per, per)], s_p4, r_p4)
+
+    def red_at(c, x):
+        return red.at[pl.ds(c * per_c + x * per, per)]
+
+    x_p4 = Exchange(g_x, sems, lambda t: seqs, lambda k: red_at(core, k))
     x_p4.start()
-    red[pl.ds(res_me * per, per)] = seqs[...]
+    mate_own = Exchange(g_core, sems, lambda t: seqs, lambda k: red_at(k, ex))
+    mate_own.start()
+    red_at(core, ex)[...] = seqs[...]
+    mates_red = []
+    for x in steps:
+        x_p4.wait_from(x)
+        mates_red.append(
+            Exchange(g_core, sems, lambda t, x=x: red_at(core, x), lambda k, x=x: red_at(k, x))
+        )
+        mates_red[-1].start()
 
     x_edge.wait_recv()
     edge = edge_in[0]
@@ -336,7 +479,9 @@
     for j in range(own):
         edge_out[pl.ds(j, own, stride=own), :] = edge[:, j * wide : (j + 1) * wide] + bias[...]
 
-    x_p4.wait_recv()
+    mate_own.wait_recv()
+    for mate in mates_red:
+        mate.wait_recv()
     for h in range(hid):
         fin_out[h * hid : (h + 1) * hid, :] = red[:, h // 4, :, (h % 4) * wide : (h % 4 + 1) * wide].reshape(hid, wide)
     for h in range(2):
@@ -344,13 +489,17 @@
         gl_out[:, lanes] = red[:, h, :, 4 * wide :].reshape(hid, wide)
         gr_out[:, lanes] = red[:, 2 + h, :, 4 * wide :].reshape(hid, wide)
     gb_out[...] = red[0, 4, :, 4 * wide :]
-    for x in (x_cot, x_left, x_gls, x_edge, x_big, x_small, x_p2, x_p3, x_p4):
-        x.wait_send()
-
-
-def seq_chunk(per, ns):
-    quads = max(1, 8 // ns)
-    return per * 8 // (ns * quads), quads
+    for sent in (
+        x_cot, left_xs, left_ys, left_own, *left_far, *left_mates, *left_mates_x,
+        *sum(left_mates_far, []), *mate_gls.values(), *x_gls, y_gls, x_edge, core_big,
+        core_small, x_big, x_small, x_p2, x_p3, x_p4, mate_own, *mates_red,
+    ):
+        sent.wait_send()
+
+
+def far_chunk(per, members):
+    quads = max(1, 8 // members)
+    return per * 8 // (members * quads), quads
 
 
 def to_tiles(x):
@@ -369,8 +518,11 @@
     hid = wl.shape[1]
     wide = fin.shape[1]
     flat = own * depth
-    per = hid // nr
-    few, quads = seq_chunk(per, ns)
+    yn, xn, cn = RES
+    per_c = hid // cn
+    per = per_c // xn
+    far = yn * ns
+    few, quads = far_chunk(per, far)
     v = pltpu.VMEM
     k = hid * depth
     n = own * wide
@@ -393,16 +545,20 @@
         v((nr * own, k), BF16), v((nr * own, k), BF16), v((k, nr * own), BF16), v((k, nr * own), BF16),
         v((own, n), F32), v((ns * own, n), F32), v((ns * own, n), BF16), v((ns * own, n), BF16),
         v((hid * hid, wide), BF16), v((hid * hid, wide), BF16), v((k, n), BF16), v((k, n), BF16),
-        v((nr * own, k), F32), v((nr, own, k), F32), v((ns * own, n), F32), v((ns, own, n), F32),
+        v((nr * own, k), F32), v((yn * xn, own, k), F32), v((yn * xn, own, k), F32),
+        v((yn * xn, own, k), F32), v((yn, own, k), F32), v((yn, own, k), F32),
+        v((ns * own, n), F32), v((ns, own, n), F32),
         v((flat, 2 * wide), BF16), v((flat, 2 * wide), BF16), v((flat, 2 * hid), F32), v((flat, hid), F32),
         v((flat, hid), F32), v((flat, chan), F32),
-        v((hid, 8, 1, 4 * wide), F32), v((nr, per, 8, 1, 4 * wide), F32),
-        v((hid, 8, 1, wide), F32), v((nr, per, 8, 1, wide), F32),
-        v((per, 8, 1, 5 * wide), F32), v((ns, few, quads, 1, 5 * wide), F32), v((few, quads, 1, 5 * wide), F32),
+        v((hid, 8, 1, 4 * wide), F32), v((per_c, 8, 1, 4 * wide), F32),
+        v((per_c, 8, 1, 4 * wide), F32), v((xn, per, 8, 1, 4 * wide), F32),
+        v((hid, 8, 1, wide), F32), v((per_c, 8, 1, wide), F32),
+        v((per_c, 8, 1, wide), F32), v((xn, per, 8, 1, wide), F32),
+        v((per, 8, 1, 5 * wide), F32), v((far, few, quads, 1, 5 * wide), F32),
+        v((few, quads, 1, 5 * wide), F32),
         v((per, 8, 1, 5 * wide), F32), v((hid, 8, 1, 5 * wide), F32),
+        pltpu.SemaphoreType.DMA((SEMS,)), pltpu.SemaphoreType.DMA((SEMS,)),
     ]
-    for axis in (ns, ns, nr, nr, nr, nr, ns, ns, nr, nr, nr, nr, ns, ns, ns, ns, nr, nr):
-        scratch.append(pltpu.SemaphoreType.DMA((axis,)))
     spec = pl.BlockSpec(memory_space=pltpu.MemorySpace.VMEM)
     edge, cols, rows, g_fin, g_wl, g_wr, g_bias = pl.pallas_call(
         functools.partial(kernel, own=own, depth=depth, hid=hid, wide=wide),

time: 93.4 us -> 92.7 us (level)
  no operation moved by 1% of the time
where the time goes in v2:
time: 92.7 us; the launch traced here: 92.4 us
  Pallas kernels  85 us (92%)
  local copies, waits for them, and re-layouts  6.8 us (7%)
    pallas_call x1, Pallas kernels, body(): pl.pallas_call(functools.partial(kernel, own=own, depth=depth, hid=hid, w...  85 us
    unnamed x17, local copies, waits for them, and re-layouts  6.8 us

profile of v2, /device:TPU:1, one launch (start us, length us, event | category | flops | bytes accessed | tf_op | source)
XLA Modules:
  0.0 92.4 jit_solution(10106647461525445186)
XLA Ops:
  0.6 85.0 %outer_mean.1 = (f32[64,128]{1,0:T(8,128)}, f32[1024,128]{1,0:T(8,128)}, f32[1024,128]{1,0:T(8,128)}, f32[1024,128]{1,0:T(8,128)}, f32[32,256]{1,0:T(8,128)}, /*index=5*/f32[32,256]{1,0:T(8,128)}, f32[1,128]{1,0:T(1,128)}) custom-call(f32[1024,128]{1,0:T(8,128)} %bitcast.28, f32[1024,128]{1,0:T(8,128)} %bitcast.29, f32[32,256]{1,0:T(8,128)} %bitcast.32, ...), custom_call_target="tpu_custom_call" | custom-call | tf_op jit(solution)/shard_map/outer_mean/pallas_call | solution.py:563
  85.6 1.4 %copy.21 = f32[8,8,128]{2,1,0:T(8,128)} copy(f32[8,8,128]{2,1,0:T(8,128)} %bitcast.37) | data formatting | bytes 65536
  87.0 0.0 copy-start.1
  87.0 1.9 %copy.22 = f32[64,8,256]{2,1,0:T(8,128)} copy(f32[64,8,256]{2,1,0:T(8,128)} %bitcast.31) | data formatting | bytes 1048576
  88.9 0.0 copy-done.1
  88.9 0.0 copy-start.3
  88.9 0.0 copy-start
  89.0 0.8 copy.23
  89.7 0.0 copy-done.3
  89.7 0.0 copy-start.2
  89.7 0.6 copy.24
  90.4 0.2 copy-done.2
  90.5 0.6 copy.25
  91.1 0.0 copy-done
  91.1 0.0 copy-start.4
  91.1 0.8 copy.26
  91.9 0.0 copy-done.4
  91.9 0.5 copy.27
Async XLA Ops:
  87.0 1.9 %copy-start.1 = (f32[1024,128]{1,0:T(8,128)S(1)}, f32[1024,128]{1,0:T(8,128)}, u32[]{:S(2)}) copy-start(f32[1024,128]{1,0:T(8,128)} %get-tuple-element.16) | copy-start | bytes 1572868
  88.9 0.8 copy-start.3
  88.9 2.2 %copy-start = (f32[1024,128]{1,0:T(8,128)S(1)}, f32[1024,128]{1,0:T(8,128)}, u32[]{:S(2)}) copy-start(f32[1024,128]{1,0:T(8,128)} %get-tuple-element.33) | copy-start | bytes 1572868
  89.7 0.8 copy-start.2
  91.1 0.8 copy-start.4

commit v3 on v2

v3 whole, which is shorter than its diff:
```python
import functools

import jax
import jax.numpy as jnp
from jax import lax
from jax.experimental import pallas as pl
from jax.experimental.pallas import tpu as pltpu
from jax.sharding import PartitionSpec as P

EPS = 1e-05
RES = (2, 4, 2)
SEMS = 72
F32 = jnp.float32
BF16 = jnp.bfloat16
MESH = pl.DeviceIdType.MESH
NN = (((1,), (0,)), ((), ()))
NT = (((1,), (1,)), ((), ()))


def mm(a, b, dims=NN):
    return lax.dot_general(a, b, dims, preferred_element_type=F32)


def split(x):
    high = x.astype(BF16)
    return high, (x - high.astype(F32)).astype(BF16)


def mm3(a, b, dims=NN):
    rows = a[0].shape[0]
    both = mm(jnp.concatenate(a, axis=0), b[0], dims)
    return both[:rows] + (both[rows:] + mm(a[0], b[1], dims))


class Group:
    def __init__(self, size, me, id_of):
        self.size = size
        self.me = me
        self.id_of = id_of

    def each(self, act):
        def one(step, _):
            act(lax.rem(self.me + step, self.size))
            return 0

        if self.size > 1:
            lax.fori_loop(1, self.size, one, 0)


class Semaphores:
    def __init__(self, ref):
        self.ref = ref
        self.used = 0

    def take(self, count=1):
        self.used += count
        return self.used - count


class Exchange:
    def __init__(self, group, sems, src_of, dst_of, bulk=None, single=False, share=None):
        self.group = group
        self.sems = sems
        self.src_of = src_of
        self.dst_of = dst_of
        self.bulk = bulk
        self.single = single
        if share is None:
            self.sent = sems.take()
            self.came = sems.take(group.size if single else 1)
        else:
            self.sent = share.sent
            self.came = sems.take(group.size) if single else share.came

    def describe(self, src, dst, slot, peer):
        return pltpu.make_async_remote_copy(
            src_ref=src,
            dst_ref=dst,
            send_sem=self.sems.ref.at[self.sent],
            recv_sem=self.sems.ref.at[self.came + slot if self.single else self.came],
            device_id=self.group.id_of(peer),
            device_id_type=MESH,
        )

    def start_to(self, peer):
        me = self.group.me
        self.describe(self.src_of(peer), self.dst_of(me), me, peer).start()

    def start(self):
        self.group.each(self.start_to)

    def wait_from(self, peer):
        self.describe(self.src_of(peer), self.dst_of(peer), peer, peer).wait_recv()

    def wait_recv(self):
        if self.group.size > 1:
            self.describe(self.bulk, self.bulk, 0, self.group.me).wait_recv()

    def wait_send(self):
        if self.group.size > 1:
            self.describe(self.bulk, self.bulk, 0, self.group.me).wait_send()


def signal_peers(groups):
    barrier = pltpu.get_barrier_semaphore()
    for group in groups:

        def signal(peer, group=group):
            pl.semaphore_signal(
                barrier, inc=1, device_id=group.id_of(peer), device_id_type=MESH
            )

        group.each(signal)


def wait_peers(groups):
    total = sum(group.size - 1 for group in groups)
    pl.semaphore_wait(pltpu.get_barrier_semaphore(), total)


def block(index, rows):
    return pl.ds(pl.multiple_of(index * rows, rows), rows)


def norm_rows(x_ref, normed, inverse, own, depth):
    def one(i, _):
        x = jnp.concatenate(
            [x_ref[pl.ds(i + p * own, depth, stride=2 * own), :] for p in range(2)], axis=1
        )
        centred = x - jnp.mean(x, axis=-1, keepdims=True)
        inv = lax.rsqrt(jnp.mean(centred * centred, axis=-1, keepdims=True) + EPS)
        normed[block(i, depth), :] = centred * inv
        inverse[block(i, depth), :] = inv
        return 0

    lax.fori_loop(0, own, one, 0)


def norm_back(upstream, normed, inverse, out_ref, own, depth):
    for i in range(own):
        rows = slice(i * depth, (i + 1) * depth)
        u = upstream[rows, :]
        y = normed[rows, :]
        first = jnp.mean(u, axis=-1, keepdims=True)
        second = jnp.mean(u * y, axis=-1, keepdims=True)
        g = inverse[rows, :] * (u - first - y * second)
        for p in range(2):
            lanes = slice(p * 128, (p + 1) * 128)
            out_ref[pl.ds(i + p * own, depth, stride=2 * own), :] = g[:, lanes]


def kernel(
    src_in, tgt_in, wl_in, wr_in, fin_in, bias_in, cot_in,
    edge_res, cols_res, rows_res, fin_res, gl_res, gr_res, gb_res,
    src, tgt, wl_t, wr_t, fin, bias, cot,
    edge_out, cols_out, rows_out, fin_out, gl_out, gr_out, gb_out,
    xs, xs_inv, xt, xt_inv, turn, left_blk, left_all, left_hl, lt_h, lt_l,
    cot_blk, cot_all, cot_hl, cot_t, fin_h, fin_l, b_h, b_l,
    gls_part, gls_c, gls_1, gls_x, gls_2, gls_y,
    edge_part, edge_in, da_h, da_l, db_h, db_l, acc64, acc32, grs_ref, up,
    big, big_c, big_1, big_x, small, small_c, small_1, small_x,
    big_2, big_far, big_3, big_s, big_r, small_2, small_far, small_3, small_s, small_r,
    in_sem, out_sem, comm_sem,
    *, own, depth, hid, wide,
):
    nr = lax.axis_size("res")
    ns = lax.axis_size("seq")
    res_me = lax.axis_index("res")
    seq_me = lax.axis_index("seq")
    scale = 1.0 / (depth * ns)
    pairs = hid // 2
    half = depth
    tile = 2 * depth
    full = own * nr
    yn, xn, cn = RES
    core = lax.rem(res_me, cn)
    ex = lax.rem(res_me // cn, xn)
    wy = res_me // (cn * xn)
    others = [lax.rem(wy + d, yn) for d in range(1, yn)]
    near = sorted(range(1, xn), key=lambda d: min(d, xn - d))
    steps = [lax.rem(ex + d, xn) for d in near]

    def res_id(y, x, c):
        return (y * xn + x) * cn + c

    g_core = Group(cn, core, lambda m: {"res": res_id(wy, ex, m)})
    g_x = Group(xn, ex, lambda m: {"res": res_id(wy, m, core)})
    g_y = Group(yn, wy, lambda m: {"res": res_id(m, ex, core)})
    g_seq = Group(ns, seq_me, lambda m: {"seq": m})
    g_far = Group(
        yn * ns, wy * ns + seq_me, lambda m: {"res": res_id(m // ns, ex, core), "seq": lax.rem(m, ns)}
    )
    greeted = (g_core, g_x, g_far)
    sems = Semaphores(comm_sem)
    loads = [
        pltpu.make_async_copy(a, b, in_sem.at[n])
        for n, (a, b) in enumerate(
            zip(
                (src_in, wl_in, cot_in, tgt_in, wr_in, fin_in, bias_in),
                (src, wl_t, cot, tgt, wr_t, fin, bias),
            )
        )
    ]
    for load in loads:
        load.start()
    signal_peers(greeted)
    for load in loads[:3]:
        load.wait()

    norm_rows(src, xs, xs_inv, own, depth)
    wl_ts = split(wl_t[...])
    left_t = mm3(wl_ts, split(xs[...]), NT)
    low = lax.broadcasted_iota(jnp.int32, (hid, tile), 1) < half
    for u in range(own // 2):
        a = left_t[:, u * tile : (u + 1) * tile]
        b = pltpu.roll(a, half, 1)
        turn[2 * u * hid : (2 * u + 1) * hid, :] = jnp.where(low, a, b)
        turn[(2 * u + 1) * hid : (2 * u + 2) * hid, :] = jnp.where(low, b, a)
    low8 = lax.broadcasted_iota(jnp.int32, (own, tile), 1) < half
    for t in range(pairs):
        even = turn[pl.ds(2 * t, own, stride=hid), :]
        odd = turn[pl.ds(2 * t + 1, own, stride=hid), :]
        left_blk[:, t * tile : (t + 1) * tile] = jnp.where(low8, even, odd)
    for j in range(own):
        cot_blk[:, j * wide : (j + 1) * wide] = cot[pl.ds(j, own, stride=own), :]

    wait_peers(greeted)

    def left_at(y, x, c):
        return left_all.at[block(res_id(y, x, c), own)]

    x_cot = Exchange(
        g_seq, sems, lambda t: cot_blk, lambda k: cot_all.at[block(k, own)],
        cot_all.at[: (ns - 1) * own],
    )
    left_xs = Exchange(
        g_x, sems, lambda t: left_blk, lambda k: left_at(wy, k, core),
        left_all.at[: (xn - 1) * own], single=True,
    )
    left_ys = Exchange(
        g_y, sems, lambda t: left_blk, lambda k: left_at(k, ex, core),
        left_all.at[: (yn - 1) * own],
    )
    left_far = [
        Exchange(
            g_x, sems, lambda t, y=y: left_at(y, ex, core), lambda k, y=y: left_at(y, k, core),
            left_all.at[: (xn - 1) * own], single=True,
        )
        for y in others
    ]
    left_own = Exchange(
        g_core, sems, lambda t: left_blk, lambda k: left_at(wy, ex, k),
        left_all.at[: yn * xn * own],
    )

    def to_core(y, x):
        return Exchange(
            g_core, sems, lambda t: left_at(y, x, core), lambda k: left_at(y, x, k), share=left_own
        )

    left_mates = [to_core(y, ex) for y in others]
    left_mates_x = [to_core(wy, x) for x in steps]
    left_mates_far = [[to_core(y, x) for x in steps] for y in others]
    left_ys.start()
    left_xs.start()
    left_own.start()
    x_cot.start()
    cot_all[block(seq_me, own), :] = cot_blk[...]
    left_all[block(res_me, own), :] = left_blk[...]

    for load in loads[3:]:
        load.wait()
    norm_rows(tgt, xt, xt_inv, own, depth)
    wr_ts = split(wr_t[...])
    right = mm3(split(xt[...]), wr_ts, NT) * scale
    right_h, right_l = split(right)
    right_k = jnp.concatenate([right_h, right_h, right_l], axis=1)
    rt_h, rt_l = split(right.T)
    left_ys.wait_recv()
    for far, mate in zip(left_far, left_mates):
        far.start()
        mate.start()
    rt_hl = jnp.concatenate([rt_h, rt_l], axis=0)
    fh, fl = split(fin[...])
    fin_h[...] = fh
    fin_l[...] = fl

    def make_b(hp, _):
        def stacked(p):
            rows = block(2 * hp + p, hid)
            return jnp.concatenate([fin_h[rows, :], fin_l[rows, :], fin_h[rows, :]], axis=0)

        weights = jnp.concatenate([stacked(0), stacked(1)], axis=1)
        for j in range(own):
            val = mm(right_k[j * depth : (j + 1) * depth], weights)
            vh, vl = split(val)
            for p in range(2):
                rows = block(2 * hp + p, depth)
                lanes = slice(p * wide, (p + 1) * wide)
                b_h[rows, j * wide : (j + 1) * wide] = vh[:, lanes]
                b_l[rows, j * wide : (j + 1) * wide] = vl[:, lanes]
        return 0

    lax.fori_loop(0, pairs, make_b, 0)
    for x, mate in zip(steps, left_mates_x):
        left_xs.wait_from(x)
        mate.start()
    for far, mates in zip(left_far, left_mates_far):
        for x, mate in zip(steps, mates):
            far.wait_from(x)
            mate.start()

    x_cot.wait_recv()
    ch, cl = split(cot_all[...])
    rows_all = ns * own
    cot_hl[:rows_all, :] = ch
    cot_hl[rows_all:, :] = cl
    cot_h = cot_hl.at[:rows_all]
    cot_l = cot_hl.at[rows_all:]
    for j in range(own):
        rows = slice(j * wide, (j + 1) * wide)
        th, tl = split(cot_all[:, rows].T)
        cot_t[rows, :rows_all] = th
        cot_t[rows, rows_all:] = tl

    def make_gls(n, _):
        rows = block(n, 2 * tile)
        y = mm(b_h[rows, :], cot_t[...])
        val = y[:, :rows_all] + (y[:, rows_all:] + mm(b_l[rows, :], cot_t[:, :rows_all]))
        gls_part[:, block(n, 2 * tile)] = val.T
        return 0

    lax.fori_loop(0, hid * depth // (2 * tile), make_gls, 0)

    def gls_at(y, x, c):
        return gls_part.at[block(res_id(y, x, c), own)]

    ys = [wy, *others]
    xs_of = [ex, *steps]
    order = [(dy, dx) for dx in [*range(xn - 1, 0, -1), 0] for dy in [*range(1, yn), 0]]
    mate_gls = {}
    first_gls = None
    for dy, dx in order:
        mate_gls[dy, dx] = Exchange(
            g_core,
            sems,
            lambda t, y=ys[dy], x=xs_of[dx]: gls_at(y, x, t),
            lambda k, y=ys[dy], x=xs_of[dx]: gls_c.at[y * xn + x],
            gls_c,
            single=True,
            share=first_gls,
        )
        first_gls = first_gls or mate_gls[dy, dx]
        mate_gls[dy, dx].start()
    x_gls = [
        Exchange(
            g_x, sems, lambda t, y=y: gls_1.at[y * xn + t], lambda k, y=y: gls_x.at[y * xn + k],
            gls_x.at[: xn - 1],
        )
        for y in ys
    ]

    def pass_gls(some):
        for dy, dx in some:
            if cn > 1:
                mate_gls[dy, dx].wait_from(cn - 1 - core)
            at = ys[dy] * xn + xs_of[dx]
            mine = gls_at(ys[dy], xs_of[dx], core)[...]
            gls_1[at] = mine + gls_c[at] if cn > 1 else mine
            if dx:
                x_gls[dy].start_to(xs_of[dx])

    left_own.wait_recv()
    for t in range(pairs):
        lanes = slice(t * tile, (t + 1) * tile)
        val = left_all[:, lanes]
        lh, ll = split(val)
        left_hl[:full, lanes] = lh
        left_hl[full:, lanes] = ll
        th, tl = split(val.T)
        lt_h[lanes, :] = th
        lt_l[lanes, :] = tl

    tiles = own // 2
    sendable = yn * (xn - 1)
    shares = [-(-sendable * n // tiles) for n in range(tiles + 1)]
    for n in range(tiles):
        cols = slice(2 * n * wide, 2 * (n + 1) * wide)
        y = mm(left_hl[...], b_h[:, cols])
        edge_part[:, cols] = y[:full] + (y[full:] + mm(left_hl[:full], b_l[:, cols]))
        pass_gls(order[shares[n] : shares[n + 1]])
    x_edge = Exchange(
        g_seq, sems, lambda t: edge_part.at[block(t, own)], lambda k: edge_in.at[k],
        edge_in.at[: ns - 1],
    )
    x_edge.start()
    edge_in[seq_me] = edge_part[block(seq_me, own), :]

    acc64[...] = jnp.zeros_like(acc64)
    acc32[...] = jnp.zeros_like(acc32)

    def make_db(q, dst_h, dst_l):
        a_h = lt_h[block(q, 2 * tile), :]
        a_hl = jnp.concatenate([a_h, lt_l[block(q, 2 * tile), :]], axis=1)
        for jj in range(own // 2):
            cols = slice(2 * jj * wide, 2 * (jj + 1) * wide)
            c_h = cot_h[:, cols]
            val = mm(a_hl, jnp.concatenate([c_h, c_h], axis=0)) + mm(a_h, cot_l[:, cols])
            vh, vl = split(val)
            for r in range(2):
                rows = slice((2 * jj + r) * depth, (2 * jj + r + 1) * depth)
                lanes = slice(r * wide, (r + 1) * wide)
                for p in range(4):
                    part = slice(p * depth, (p + 1) * depth)
                    dst_h[rows, p * wide : (p + 1) * wide] = vh[part, lanes]
                    dst_l[rows, p * wide : (p + 1) * wide] = vl[part, lanes]

    def use_db(q, src_h, src_l):
        dh = src_h[...]
        dl = src_l[...]
        y = mm(rt_hl, dh)
        grad = y[:hid, :] + (y[hid:, :] + mm(rt_h, dl))
        big[:, q, :, :] = grad.reshape(hid, 1, 4 * wide)

        def flat(ref):
            return jnp.concatenate([ref[block(4 * q + p, hid), :] for p in range(4)], axis=1)

        f_h = flat(fin_h)
        acc64[...] += mm(dh, jnp.concatenate([f_h, flat(fin_l)], axis=0), NT)
        acc32[...] += mm(dl, f_h, NT)

    def two_db(t, _):
        make_db(2 * t + 1, db_h, db_l)
        use_db(2 * t, da_h, da_l)
        make_db(2 * t + 2, da_h, da_l)
        use_db(2 * t + 1, db_h, db_l)
        return 0

    quads = hid // 4
    make_db(0, da_h, da_l)
    lax.fori_loop(0, 1, two_db, 0)
    pass_gls(order[sendable:])
    lax.fori_loop(1, quads // 2 - 1, two_db, 0)
    make_db(quads - 1, db_h, db_l)
    use_db(quads - 2, da_h, da_l)
    use_db(quads - 1, db_h, db_l)
    per_c = hid // cn
    per = per_c // xn

    def start_core(whole, mine):
        out = Exchange(g_core, sems, lambda t: whole.at[pl.ds(t * per_c, per_c)], lambda k: mine, mine)
        out.start()
        return out

    def fold_core(exchange, whole, other, total):
        exchange.wait_recv()
        if cn > 1:
            total[...] = whole[pl.ds(core * per_c, per_c)] + other[...]
        else:
            total[...] = whole[...]

    def start_x(total, arrived):
        out = Exchange(
            g_x, sems, lambda t: total.at[pl.ds(t * per, per)], lambda k: arrived.at[k],
            arrived.at[: xn - 1],
        )
        out.start()
        arrived[ex] = total[pl.ds(ex * per, per)]
        return out

    core_big = start_core(big, big_c)

    both = acc64[...]
    grs = (both[:, :hid] + both[:, hid:] + acc32[...]) * scale
    xts = split(xt[...])
    gr_t = mm3(split(grs.T), xts)
    gb = jnp.sum(cot[...], axis=0, keepdims=True)
    for h in range(2):
        small[:, 2 + h, :, :] = gr_t[:, h * wide : (h + 1) * wide].reshape(hid, 1, wide)
    small[:, 4, :, :] = jnp.broadcast_to(gb, (hid, wide)).reshape(hid, 1, wide)
    for h in range(5, 8):
        small[:, h, :, :] = jnp.zeros((hid, 1, wide), F32)

    def fold_x(y, arriving):
        arriving.wait_recv()
        total = gls_1[y * xn + ex]
        for x in steps:
            total = total + gls_x[y * xn + x]
        return total

    y_gls = Exchange(
        g_y, sems, lambda t: gls_2.at[t], lambda k: gls_y.at[k], gls_y.at[: yn - 1]
    )
    for y, arriving in zip(others, x_gls[1:]):
        gls_2[y] = fold_x(y, arriving)
        y_gls.start_to(y)
    gls = fold_x(wy, x_gls[0])
    fold_core(core_big, big, big_c, big_1)
    x_big = start_x(big_1, big_x)
    stores = []

    def store(value, result):
        stores.append(pltpu.make_async_copy(value, result, out_sem.at[len(stores)]))
        stores[-1].start()

    up[...] = mm3(split(grs), wr_ts)
    norm_back(up, xt, xt_inv, cols_out, own, depth)
    store(cols_out, cols_res)
    y_gls.wait_recv()
    for y in others:
        gls = gls + gls_y[y]
    for t in range(pairs):
        v = gls[:, t * tile : (t + 1) * tile]
        turn[pl.ds(2 * t, own, stride=hid), :] = v
        turn[pl.ds(2 * t + 1, own, stride=hid), :] = pltpu.roll(v, half, 1)
    parts = []
    for u in range(own // 2):
        a = turn[2 * u * hid : (2 * u + 1) * hid, :]
        b = turn[(2 * u + 1) * hid : (2 * u + 2) * hid, :]
        parts.append(jnp.where(low, a, pltpu.roll(b, half, 1)))
    gls_t = jnp.concatenate(parts, axis=1)
    gl_t = mm3(split(gls_t), split(xs[...]))
    for h in range(2):
        small[:, h, :, :] = gl_t[:, h * wide : (h + 1) * wide].reshape(hid, 1, wide)
    core_small = start_core(small, small_c)

    span_rows, span = far_chunk(per, g_far.size)
    groups = 8 // span

    def at(ref, t):
        return ref.at[
            pl.ds((t // groups) * span_rows, span_rows), pl.ds(lax.rem(t, groups) * span, span)
        ]

    def start_far(exchange, arrived, total, parts):
        exchange.wait_recv()
        total[...] = jnp.sum(arrived[...], axis=0)
        out = Exchange(
            g_far, sems, lambda t: at(total, t), lambda k: parts.at[k], parts.at[: g_far.size - 1]
        )
        out.start()
        parts[g_far.me] = at(total, g_far.me)[...]
        return out

    def start_back(exchange, parts, mine, whole):
        exchange.wait_recv()
        mine[...] = jnp.sum(parts[...], axis=0)
        out = Exchange(
            g_far, sems, lambda t: mine, lambda k: at(whole, k), parts.at[: g_far.size - 1]
        )
        out.start()
        at(whole, g_far.me)[...] = mine[...]
        return out

    def red_at(red, c, x):
        return red.at[pl.ds(c * per_c + x * per, per)]

    def start_wide(exchange, whole, red):
        exchange.wait_recv()
        out = Exchange(
            g_x, sems, lambda t: whole, lambda k: red_at(red, core, k),
            red.at[: (xn - 1) * per], single=True,
        )
        out.start()
        mate = Exchange(
            g_core, sems, lambda t: whole, lambda k: red_at(red, k, ex), red.at[: xn * per]
        )
        mate.start()
        red_at(red, core, ex)[...] = whole[...]
        return out, mate

    def start_mates(wide_pair, red):
        out, mate = wide_pair
        for x in steps:
            out.wait_from(x)
            Exchange(
                g_core,
                sems,
                lambda t, x=x: red_at(red, core, x),
                lambda k, x=x: red_at(red, k, x),
                share=mate,
            ).start()

    far_big = start_far(x_big, big_x, big_2, big_far)
    up[...] = mm3(split(gls_t.T), wl_ts)
    norm_back(up, xs, xs_inv, rows_out, own, depth)
    store(rows_out, rows_res)
    fold_core(core_small, small, small_c, small_1)
    x_small = start_x(small_1, small_x)

    x_edge.wait_recv()
    edge = edge_in[0]
    for k in range(1, ns):
        edge = edge + edge_in[k]
    for j in range(own):
        edge_out[pl.ds(j, own, stride=own), :] = edge[:, j * wide : (j + 1) * wide] + bias[...]
    store(edge_out, edge_res)

    back_big = start_back(far_big, big_far, big_3, big_s)
    far_small = start_far(x_small, small_x, small_2, small_far)
    for sent in (
        x_cot, left_xs, left_ys, left_own, *left_far, first_gls, *x_gls, y_gls, x_edge,
        core_big, core_small, x_big, x_small, far_big,
    ):
        sent.wait_send()
    wide_big = start_wide(back_big, big_s, big_r)
    back_small = start_back(far_small, small_far, small_3, small_s)
    start_mates(wide_big, big_r)
    wide_big[1].wait_recv()
    for h in range(hid):
        fin_out[h * hid : (h + 1) * hid, :] = big_r[
            :, h // 4, :, (h % 4) * wide : (h % 4 + 1) * wide
        ].reshape(hid, wide)
    store(fin_out, fin_res)
    wide_small = start_wide(back_small, small_s, small_r)
    start_mates(wide_small, small_r)
    for sent in (far_small, back_big, back_small, *wide_big):
        sent.wait_send()
    wide_small[1].wait_recv()
    for h in range(2):
        lanes = slice(h * wide, (h + 1) * wide)
        gl_out[:, lanes] = small_r[:, h].reshape(hid, wide)
        gr_out[:, lanes] = small_r[:, 2 + h].reshape(hid, wide)
    gb_out[...] = small_r[0, 4]
    store(gl_out, gl_res)
    store(gr_out, gr_res)
    store(gb_out, gb_res)
    for sent in wide_small:
        sent.wait_send()
    for put in stores:
        put.wait()
    assert sems.used <= SEMS, sems.used


def copy_kernel(*refs):
    count = (len(refs) - 2) // 3
    ins, outs, bufs = refs[:count], refs[count : 2 * count], refs[2 * count : 3 * count]
    sem_in, sem_out = refs[-2:]
    gets = [pltpu.make_async_copy(a, b, sem_in.at[n]) for n, (a, b) in enumerate(zip(ins, bufs))]
    puts = [pltpu.make_async_copy(b, o, sem_out.at[n]) for n, (b, o) in enumerate(zip(bufs, outs))]
    for get in gets:
        get.start()
    for get, put in zip(gets, puts):
        get.wait()
        put.start()
    for put in puts:
        put.wait()


def copy_out(arrays):
    anywhere = pl.BlockSpec(memory_space=pl.ANY)
    return pl.pallas_call(
        copy_kernel,
        out_shape=tuple(jax.ShapeDtypeStruct(a.shape, a.dtype) for a in arrays),
        in_specs=[anywhere] * len(arrays),
        out_specs=(anywhere,) * len(arrays),
        scratch_shapes=[pltpu.VMEM(a.shape, a.dtype) for a in arrays]
        + [pltpu.SemaphoreType.DMA((len(arrays),))] * 2,
        name="copy_out",
    )(*arrays)


def far_chunk(per, members):
    quads = max(1, 8 // members)
    return per * 8 // (members * quads), quads


def to_tiles(x):
    depth, own, chan = x.shape
    return x.reshape(depth, own, 2, chan // 2).swapaxes(1, 2).reshape(-1, chan // 2)


def from_tiles(x, depth, own):
    return x.reshape(depth, 2, own, -1).swapaxes(1, 2).reshape(depth, own, -1)


def body(tgt, src, wl, wr, fin, bias, cot):
    ns = lax.axis_size("seq")
    nr = lax.axis_size("res")
    depth, own, chan = src.shape
    hid = wl.shape[1]
    wide = fin.shape[1]
    flat = own * depth
    yn, xn, cn = RES
    per_c = hid // cn
    per = per_c // xn
    far = yn * ns
    few, quads = far_chunk(per, far)
    v = pltpu.VMEM
    k = hid * depth
    n = own * wide
    operands = (
        to_tiles(src), to_tiles(tgt), wl.T, wr.T, fin,
        bias.reshape(1, wide), cot.reshape(own * own, wide),
    )
    outs = (
        jax.ShapeDtypeStruct((own * own, wide), F32),
        jax.ShapeDtypeStruct((2 * flat, 128), F32),
        jax.ShapeDtypeStruct((2 * flat, 128), F32),
        jax.ShapeDtypeStruct((hid * hid, wide), F32),
        jax.ShapeDtypeStruct((hid, chan), F32),
        jax.ShapeDtypeStruct((hid, chan), F32),
        jax.ShapeDtypeStruct((1, wide), F32),
    )
    scratch = [v(a.shape, F32) for a in (*operands, *outs)] + [
        v((flat, chan), F32), v((flat, 1), F32), v((flat, chan), F32), v((flat, 1), F32),
        v((own * hid, 2 * depth), F32), v((own, k), F32), v((nr * own, k), F32),
        v((2 * nr * own, k), BF16), v((k, nr * own), BF16), v((k, nr * own), BF16),
        v((own, n), F32), v((ns * own, n), F32), v((2 * ns * own, n), BF16), v((n, 2 * ns * own), BF16),
        v((hid * hid, wide), BF16), v((hid * hid, wide), BF16), v((k, n), BF16), v((k, n), BF16),
        v((nr * own, k), F32), v((yn * xn, own, k), F32), v((yn * xn, own, k), F32),
        v((yn * xn, own, k), F32), v((yn, own, k), F32), v((yn, own, k), F32),
        v((ns * own, n), F32), v((ns, own, n), F32),
        v((flat, 4 * wide), BF16), v((flat, 4 * wide), BF16), v((flat, 4 * wide), BF16),
        v((flat, 4 * wide), BF16), v((flat, 2 * hid), F32), v((flat, hid), F32),
        v((flat, hid), F32), v((flat, chan), F32),
        v((hid, 8, 1, 4 * wide), F32), v((per_c, 8, 1, 4 * wide), F32),
        v((per_c, 8, 1, 4 * wide), F32), v((xn, per, 8, 1, 4 * wide), F32),
        v((hid, 8, 1, wide), F32), v((per_c, 8, 1, wide), F32),
        v((per_c, 8, 1, wide), F32), v((xn, per, 8, 1, wide), F32),
    ]
    for lanes in (4 * wide, wide):
        scratch += [
            v((per, 8, 1, lanes), F32), v((far, few, quads, 1, lanes), F32),
            v((few, quads, 1, lanes), F32), v((per, 8, 1, lanes), F32),
            v((hid, 8, 1, lanes), F32),
        ]
    scratch += [
        pltpu.SemaphoreType.DMA((len(operands),)), pltpu.SemaphoreType.DMA((len(outs),)),
        pltpu.SemaphoreType.DMA((SEMS,)),
    ]
    spec = pl.BlockSpec(memory_space=pl.ANY)
    results = pl.pallas_call(
        functools.partial(kernel, own=own, depth=depth, hid=hid, wide=wide),
        out_shape=outs,
        in_specs=[spec] * len(operands),
        out_specs=(spec,) * len(outs),
        scratch_shapes=scratch,
        compiler_params=pltpu.CompilerParams(
            collective_id=0, has_side_effects=True, vmem_limit_bytes=60 * 2**20
        ),
        name="outer_mean",
    )(*operands)
    edge, cols, rows, g_fin, g_wl, g_wr, g_bias = copy_out(results)
    return (
        edge.reshape(own, own, wide),
        from_tiles(cols, depth, own),
        from_tiles(rows, depth, own),
        g_wl.T,
        g_wr.T,
        g_fin,
        g_bias.reshape(wide),
    )


def solution(mesh):
    parts = P("seq", "res", None)
    in_specs = (parts, parts, P(), P(), P(), P(), parts)
    out_specs = (parts, parts, parts, P(), P(), P(), P())
    return jax.shard_map(body, mesh=mesh, in_specs=in_specs, out_specs=out_specs, check_vma=False)
```

time: 92.7 us -> 77.6 us (0.84)
  Pallas kernels: 85 us -> 76.8 us
  local copies, waits for them, and re-layouts: 6.8 us -> 0 us
    pallas_call x1, Pallas kernels: 85 us -> 74.5 us  [body(): pl.pallas_call(functools.partial(kernel, own=own, depth=depth, hid=hid, w...]
    unnamed x17 -> x0, local copies, waits for them, and re-layouts: 6.8 us -> none
    pallas_call x0 -> x1, Pallas kernels: none -> 2.33 us  [copy_out(): pl.pallas_call(copy_kernel, out_shape=tuple((jax.ShapeDtypeStruct(a.shape...]
where the time goes in v3:
time: 77.6 us; the launch traced here: 77.5 us
  Pallas kernels  76.8 us (99%)
    pallas_call x1, Pallas kernels, body(): pl.pallas_call(functools.partial(kernel, own=own, depth=depth, hid=hid, w...  74.5 us
    pallas_call x1, Pallas kernels, copy_out(): pl.pallas_call(copy_kernel, out_shape=tuple((jax.ShapeDtypeStruct(a.shape...  2.33 us

profile of v3, /device:TPU:1, one launch (start us, length us, event | category | flops | bytes accessed | tf_op | source)
XLA Modules:
  0.0 77.5 jit_solution(13089817558809610847)
XLA Ops:
  0.6 74.5 %outer_mean.1 = (f32[64,128]{1,0:T(8,128)}, f32[1024,128]{1,0:T(8,128)}, f32[1024,128]{1,0:T(8,128)}, f32[1024,128]{1,0:T(8,128)}, f32[32,256]{1,0:T(8,128)}, /*index=5*/f32[32,256]{1,0:T(8,128)}, f32[1,128]{1,0:T(1,128)}) custom-call(f32[1024,128]{1,0:T(8,128)} %bitcast.28, f32[1024,128]{1,0:T(8,128)} %bitcast.29, f32[32,256]{1,0:T(8,128)} %bitcast.30, ...), custom_call_target="tpu_custom_call" | custom-call | tf_op jit(solution)/shard_map/outer_mean/pallas_call | solution.py:733
  75.1 2.3 %copy_out.1 = (f32[64,128]{1,0:T(8,128)}, f32[1024,128]{1,0:T(8,128)}, f32[1024,128]{1,0:T(8,128)}, f32[1024,128]{1,0:T(8,128)}, f32[32,256]{1,0:T(8,128)}, /*index=5*/f32[32,256]{1,0:T(8,128)}, f32[1,128]{1,0:T(1,128)}) custom-call(f32[64,128]{1,0:T(8,128)} %get-tuple-element.21.refs_0_, f32[1024,128]{1,0:T(8,128)} %get-tuple-element.22.refs_1_, ...), custom_call_target="tpu_custom_call" | custom-call | tf_op jit(solution)/shard_map/copy_out/pallas_call | solution.py:652

commit v4 on v3

--- a/solution.py
+++ b/solution.py
@@ -9,7 +9,7 @@
 
 EPS = 1e-05
 RES = (2, 4, 2)
-SEMS = 72
+SEMS = 75
 F32 = jnp.float32
 BF16 = jnp.bfloat16
 MESH = pl.DeviceIdType.MESH
@@ -324,13 +324,13 @@
         cot_t[rows, rows_all:] = tl
 
     def make_gls(n, _):
-        rows = block(n, 2 * tile)
+        rows = block(n, 8 * tile)
         y = mm(b_h[rows, :], cot_t[...])
         val = y[:, :rows_all] + (y[:, rows_all:] + mm(b_l[rows, :], cot_t[:, :rows_all]))
-        gls_part[:, block(n, 2 * tile)] = val.T
+        gls_part[:, block(n, 8 * tile)] = val.T
         return 0
 
-    lax.fori_loop(0, hid * depth // (2 * tile), make_gls, 0)
+    lax.fori_loop(0, hid * depth // (8 * tile), make_gls, 0)
 
     def gls_at(y, x, c):
         return gls_part.at[block(res_id(y, x, c), own)]
@@ -382,13 +382,10 @@
         lt_l[lanes, :] = tl
 
     tiles = own // 2
-    sendable = yn * (xn - 1)
-    shares = [-(-sendable * n // tiles) for n in range(tiles + 1)]
     for n in range(tiles):
         cols = slice(2 * n * wide, 2 * (n + 1) * wide)
         y = mm(left_hl[...], b_h[:, cols])
         edge_part[:, cols] = y[:full] + (y[full:] + mm(left_hl[:full], b_l[:, cols]))
-        pass_gls(order[shares[n] : shares[n + 1]])
     x_edge = Exchange(
         g_seq, sems, lambda t: edge_part.at[block(t, own)], lambda k: edge_in.at[k],
         edge_in.at[: ns - 1],
@@ -436,39 +433,50 @@
         use_db(2 * t + 1, db_h, db_l)
         return 0
 
+    per_c = hid // cn
+    per = per_c // xn
+
+    def start_core(whole, mine, quads):
+        out = Exchange(
+            g_core, sems, lambda t: whole.at[pl.ds(t * per_c, per_c), quads],
+            lambda k: mine.at[:, quads], mine.at[:, quads],
+        )
+        out.start()
+        return out
+
+    def fold_core(exchange, whole, other, total, quads):
+        exchange.wait_recv()
+        if cn > 1:
+            total[:, quads] = whole[pl.ds(core * per_c, per_c), quads] + other[:, quads]
+        else:
+            total[:, quads] = whole[:, quads]
+
+    def start_x(total, arrived, quads):
+        out = Exchange(
+            g_x, sems, lambda t: total.at[pl.ds(t * per, per), quads],
+            lambda k: arrived.at[k, :, quads], arrived.at[: xn - 1, :, quads],
+        )
+        out.start()
+        arrived[ex, :, quads] = total[pl.ds(ex * per, per), quads]
+        return out
+
+    halves = [pl.ds(0, 4), pl.ds(4, 4)]
+    every = pl.ds(0, 8)
     quads = hid // 4
+    pass_gls(order[:1])
     make_db(0, da_h, da_l)
-    lax.fori_loop(0, 1, two_db, 0)
-    pass_gls(order[sendable:])
-    lax.fori_loop(1, quads // 2 - 1, two_db, 0)
+    pass_gls(order[1:2])
+    for t in range(quads // 2 - 1):
+        lax.fori_loop(t, t + 1, two_db, 0)
+        pass_gls(order[2 * t + 2 : 2 * t + 4])
+        if t == quads // 4 - 1:
+            core_big = [start_core(big, big_c, halves[0])]
     make_db(quads - 1, db_h, db_l)
     use_db(quads - 2, da_h, da_l)
     use_db(quads - 1, db_h, db_l)
-    per_c = hid // cn
-    per = per_c // xn
-
-    def start_core(whole, mine):
-        out = Exchange(g_core, sems, lambda t: whole.at[pl.ds(t * per_c, per_c)], lambda k: mine, mine)
-        out.start()
-        return out
-
-    def fold_core(exchange, whole, other, total):
-        exchange.wait_recv()
-        if cn > 1:
-            total[...] = whole[pl.ds(core * per_c, per_c)] + other[...]
-        else:
-            total[...] = whole[...]
-
-    def start_x(total, arrived):
-        out = Exchange(
-            g_x, sems, lambda t: total.at[pl.ds(t * per, per)], lambda k: arrived.at[k],
-            arrived.at[: xn - 1],
-        )
-        out.start()
-        arrived[ex] = total[pl.ds(ex * per, per)]
-        return out
-
-    core_big = start_core(big, big_c)
+    core_big.append(start_core(big, big_c, halves[1]))
+    fold_core(core_big[0], big, big_c, big_1, halves[0])
+    x_big = [start_x(big_1, big_x, halves[0])]
 
     both = acc64[...]
     grs = (both[:, :hid] + both[:, hid:] + acc32[...]) * scale
@@ -495,8 +503,8 @@
         gls_2[y] = fold_x(y, arriving)
         y_gls.start_to(y)
     gls = fold_x(wy, x_gls[0])
-    fold_core(core_big, big, big_c, big_1)
-    x_big = start_x(big_1, big_x)
+    fold_core(core_big[1], big, big_c, big_1, halves[1])
+    x_big.append(start_x(big_1, big_x, halves[1]))
     stores = []
 
     def store(value, result):
@@ -522,7 +530,7 @@
     gl_t = mm3(split(gls_t), split(xs[...]))
     for h in range(2):
         small[:, h, :, :] = gl_t[:, h * wide : (h + 1) * wide].reshape(hid, 1, wide)
-    core_small = start_core(small, small_c)
+    core_small = start_core(small, small_c, every)
 
     span_rows, span = far_chunk(per, g_far.size)
     groups = 8 // span
@@ -532,8 +540,9 @@
             pl.ds((t // groups) * span_rows, span_rows), pl.ds(lax.rem(t, groups) * span, span)
         ]
 
-    def start_far(exchange, arrived, total, parts):
-        exchange.wait_recv()
+    def start_far(exchanges, arrived, total, parts):
+        for exchange in exchanges:
+            exchange.wait_recv()
         total[...] = jnp.sum(arrived[...], axis=0)
         out = Exchange(
             g_far, sems, lambda t: at(total, t), lambda k: parts.at[k], parts.at[: g_far.size - 1]
@@ -581,12 +590,12 @@
                 share=mate,
             ).start()
 
-    far_big = start_far(x_big, big_x, big_2, big_far)
     up[...] = mm3(split(gls_t.T), wl_ts)
     norm_back(up, xs, xs_inv, rows_out, own, depth)
     store(rows_out, rows_res)
-    fold_core(core_small, small, small_c, small_1)
-    x_small = start_x(small_1, small_x)
+    fold_core(core_small, small, small_c, small_1, every)
+    x_small = start_x(small_1, small_x, every)
+    far_big = start_far(x_big, big_x, big_2, big_far)
 
     x_edge.wait_recv()
     edge = edge_in[0]
@@ -596,23 +605,23 @@
         edge_out[pl.ds(j, own, stride=own), :] = edge[:, j * wide : (j + 1) * wide] + bias[...]
     store(edge_out, edge_res)
 
+    far_small = start_far([x_small], small_x, small_2, small_far)
     back_big = start_back(far_big, big_far, big_3, big_s)
-    far_small = start_far(x_small, small_x, small_2, small_far)
     for sent in (
         x_cot, left_xs, left_ys, left_own, *left_far, first_gls, *x_gls, y_gls, x_edge,
-        core_big, core_small, x_big, x_small, far_big,
+        *core_big, core_small, *x_big, x_small, far_big,
     ):
         sent.wait_send()
+    back_small = start_back(far_small, small_far, small_3, small_s)
     wide_big = start_wide(back_big, big_s, big_r)
-    back_small = start_back(far_small, small_far, small_3, small_s)
     start_mates(wide_big, big_r)
+    wide_small = start_wide(back_small, small_s, small_r)
     wide_big[1].wait_recv()
     for h in range(hid):
         fin_out[h * hid : (h + 1) * hid, :] = big_r[
             :, h // 4, :, (h % 4) * wide : (h % 4 + 1) * wide
         ].reshape(hid, wide)
     store(fin_out, fin_res)
-    wide_small = start_wide(back_small, small_s, small_r)
     start_mates(wide_small, small_r)
     for sent in (far_small, back_big, back_small, *wide_big):
         sent.wait_send()

time: 77.6 us -> 71 us (0.915)
  Pallas kernels: 76.8 us -> 70.3 us
    pallas_call x1, Pallas kernels: 74.5 us -> 67.9 us  [body(): pl.pallas_call(functools.partial(kernel, own=own, depth=depth, hid=hid, w...]
where the time goes in v4:
time: 71 us; the launch traced here: 70.9 us
  Pallas kernels  70.3 us (99%)
    pallas_call x1, Pallas kernels, body(): pl.pallas_call(functools.partial(kernel, own=own, depth=depth, hid=hid, w...  67.9 us
    pallas_call x1, Pallas kernels, copy_out(): pl.pallas_call(copy_kernel, out_shape=tuple((jax.ShapeDtypeStruct(a.shape...  2.33 us

profile of v4, /device:TPU:1, one launch (start us, length us, event | category | flops | bytes accessed | tf_op | source)
XLA Modules:
  0.0 70.9 jit_solution(13015613757528061412)
XLA Ops:
  0.6 67.9 %outer_mean.1 = (f32[64,128]{1,0:T(8,128)}, f32[1024,128]{1,0:T(8,128)}, f32[1024,128]{1,0:T(8,128)}, f32[1024,128]{1,0:T(8,128)}, f32[32,256]{1,0:T(8,128)}, /*index=5*/f32[32,256]{1,0:T(8,128)}, f32[1,128]{1,0:T(1,128)}) custom-call(f32[1024,128]{1,0:T(8,128)} %bitcast.28, f32[1024,128]{1,0:T(8,128)} %bitcast.29, f32[32,256]{1,0:T(8,128)} %bitcast.30, ...), custom_call_target="tpu_custom_call" | custom-call | tf_op jit(solution)/shard_map/outer_mean/pallas_call | solution.py:742
  68.6 2.3 %copy_out.1 = (f32[64,128]{1,0:T(8,128)}, f32[1024,128]{1,0:T(8,128)}, f32[1024,128]{1,0:T(8,128)}, f32[1024,128]{1,0:T(8,128)}, f32[32,256]{1,0:T(8,128)}, /*index=5*/f32[32,256]{1,0:T(8,128)}, f32[1,128]{1,0:T(1,128)}) custom-call(f32[64,128]{1,0:T(8,128)} %get-tuple-element.21.refs_0_, f32[1024,128]{1,0:T(8,128)} %get-tuple-element.22.refs_1_, ...), custom_call_target="tpu_custom_call" | custom-call | tf_op jit(solution)/shard_map/copy_out/pallas_call | solution.py:661

commit v5 on v4

--- a/solution.py
+++ b/solution.py
@@ -33,18 +33,20 @@
 
 
 class Group:
-    def __init__(self, size, me, id_of):
+    def __init__(self, size, me, id_of, peer=None):
         self.size = size
         self.me = me
         self.id_of = id_of
-
-    def each(self, act):
-        def one(step, _):
-            act(lax.rem(self.me + step, self.size))
+        self.plain = lambda n: lax.rem(me + 1 + n, size)
+        self.peer = peer or self.plain
+
+    def each(self, act, plain=False):
+        def one(n, _):
+            act(self.plain(n) if plain else self.peer(n))
             return 0
 
         if self.size > 1:
-            lax.fori_loop(1, self.size, one, 0)
+            lax.fori_loop(0, self.size - 1, one, 0)
 
 
 class Semaphores:
@@ -110,7 +112,7 @@
                 barrier, inc=1, device_id=group.id_of(peer), device_id_type=MESH
             )
 
-        group.each(signal)
+        group.each(signal, plain=True)
 
 
 def wait_peers(groups):
@@ -186,9 +188,23 @@
     g_core = Group(cn, core, lambda m: {"res": res_id(wy, ex, m)})
     g_x = Group(xn, ex, lambda m: {"res": res_id(wy, m, core)})
     g_y = Group(yn, wy, lambda m: {"res": res_id(m, ex, core)})
+    zn = ns // 2
+    zed = seq_me // 2
+
+    def seq_peer(k, flip):
+        turn_z = (1 - 2 * lax.rem(k, 2)) * ((k + 1) // 2)
+        return lax.rem(zed + zn + zn // 2 + turn_z, zn) * 2 + lax.rem(seq_me + flip, 2)
+
+    def far_peer(n):
+        rest = lax.rem(n + 1, 2 * yn)
+        return lax.rem(wy + rest // 2, yn) * ns + seq_peer(n // (2 * yn), lax.rem(rest, 2))
+
     g_seq = Group(ns, seq_me, lambda m: {"seq": m})
     g_far = Group(
-        yn * ns, wy * ns + seq_me, lambda m: {"res": res_id(m // ns, ex, core), "seq": lax.rem(m, ns)}
+        yn * ns,
+        wy * ns + seq_me,
+        lambda m: {"res": res_id(m // ns, ex, core), "seq": lax.rem(m, ns)},
+        far_peer,
     )
     greeted = (g_core, g_x, g_far)
     sems = Semaphores(comm_sem)
@@ -642,29 +658,25 @@
 
 
 def copy_kernel(*refs):
-    count = (len(refs) - 2) // 3
-    ins, outs, bufs = refs[:count], refs[count : 2 * count], refs[2 * count : 3 * count]
-    sem_in, sem_out = refs[-2:]
-    gets = [pltpu.make_async_copy(a, b, sem_in.at[n]) for n, (a, b) in enumerate(zip(ins, bufs))]
-    puts = [pltpu.make_async_copy(b, o, sem_out.at[n]) for n, (b, o) in enumerate(zip(bufs, outs))]
-    for get in gets:
-        get.start()
-    for get, put in zip(gets, puts):
-        get.wait()
+    count = (len(refs) - 1) // 2
+    puts = [
+        pltpu.make_async_copy(a, b, refs[-1].at[n])
+        for n, (a, b) in enumerate(zip(refs[:count], refs[count : 2 * count]))
+    ]
+    for put in puts:
         put.start()
     for put in puts:
         put.wait()
 
 
 def copy_out(arrays):
-    anywhere = pl.BlockSpec(memory_space=pl.ANY)
     return pl.pallas_call(
         copy_kernel,
         out_shape=tuple(jax.ShapeDtypeStruct(a.shape, a.dtype) for a in arrays),
-        in_specs=[anywhere] * len(arrays),
-        out_specs=(anywhere,) * len(arrays),
-        scratch_shapes=[pltpu.VMEM(a.shape, a.dtype) for a in arrays]
-        + [pltpu.SemaphoreType.DMA((len(arrays),))] * 2,
+        in_specs=[pl.BlockSpec(memory_space=pl.ANY)] * len(arrays),
+        out_specs=(pl.BlockSpec(memory_space=pltpu.MemorySpace.HBM),) * len(arrays),
+        scratch_shapes=[pltpu.SemaphoreType.DMA((len(arrays),))],
+        compiler_params=pltpu.CompilerParams(vmem_limit_bytes=2**20),
         name="copy_out",
     )(*arrays)
 
@@ -739,14 +751,15 @@
         pltpu.SemaphoreType.DMA((SEMS,)),
     ]
     spec = pl.BlockSpec(memory_space=pl.ANY)
+    operands = tuple(pltpu.with_memory_space_constraint(a, pltpu.MemorySpace.HBM) for a in operands)
     results = pl.pallas_call(
         functools.partial(kernel, own=own, depth=depth, hid=hid, wide=wide),
         out_shape=outs,
-        in_specs=[spec] * len(operands),
+        in_specs=[pl.BlockSpec(memory_space=pltpu.MemorySpace.HBM)] * len(operands),
         out_specs=(spec,) * len(outs),
         scratch_shapes=scratch,
         compiler_params=pltpu.CompilerParams(
-            collective_id=0, has_side_effects=True, vmem_limit_bytes=60 * 2**20
+            collective_id=0, has_side_effects=True, vmem_limit_bytes=36 * 2**20
         ),
         name="outer_mean",
     )(*operands)

time: 71 us -> 69.3 us (0.976)
  Pallas kernels: 70.3 us -> 68.5 us
    pallas_call x1, Pallas kernels: 2.33 us -> 1.22 us  [copy_out(): pl.pallas_call(copy_kernel, out_shape=tuple((jax.ShapeDtypeStruct(a.shape...]
where the time goes in v5:
time: 69.3 us; the launch traced here: 69.2 us
  Pallas kernels  68.5 us (99%)
    pallas_call x1, Pallas kernels, body(): pl.pallas_call(functools.partial(kernel, own=own, depth=depth, hid=hid, w...  67.3 us

profile of v5, /device:TPU:1, one launch (start us, length us, event | category | flops | bytes accessed | tf_op | source)
XLA Modules:
  0.0 69.2 jit_solution(1034292541607318199)
XLA Ops:
  0.6 67.3 %outer_mean.1 = (f32[64,128]{1,0:T(8,128)S(1)}, f32[1024,128]{1,0:T(8,128)S(1)}, f32[1024,128]{1,0:T(8,128)S(1)}, f32[1024,128]{1,0:T(8,128)S(1)}, f32[32,256]{1...) custom-call(f32[1024,128]{1,0:T(8,128)} %bitcast.28, f32[1024,128]{1,0:T(8,128)} %bitcast.29, ...), custom_call_target="tpu_custom_call" | custom-call | tf_op jit(solution)/shard_map/outer_mean/pallas_call | solution.py:755
  67.9 1.2 %copy_out.1 = (f32[64,128]{1,0:T(8,128)}, f32[1024,128]{1,0:T(8,128)}, f32[1024,128]{1,0:T(8,128)}, f32[1024,128]{1,0:T(8,128)}, f32[32,256]{1,0:T(8,128)}, /*index=5*/f32[32,256]{1,0:T(8,128)}, f32[1,128]{1,0:T(1,128)}) custom-call(f32[64,128]{1,0:T(8,128)S(1)} %get-tuple-element.21.refs_0_, f32[1024,128]{1,0:T(8,128)S(1)} %get-tuple-element.22.refs_1_, ...), custom_call_target="tpu_custom_call" | custom-call | tf_op jit(solution)/shard_map/copy_out/pallas_call | solution.py:673

commit v6 on v5

--- a/solution.py
+++ b/solution.py
@@ -9,7 +9,7 @@
 
 EPS = 1e-05
 RES = (2, 4, 2)
-SEMS = 75
+SEMS = 78
 F32 = jnp.float32
 BF16 = jnp.bfloat16
 MESH = pl.DeviceIdType.MESH
@@ -160,7 +160,7 @@
     cot_blk, cot_all, cot_hl, cot_t, fin_h, fin_l, b_h, b_l,
     gls_part, gls_c, gls_1, gls_x, gls_2, gls_y,
     edge_part, edge_in, da_h, da_l, db_h, db_l, acc64, acc32, grs_ref, up,
-    big, big_c, big_1, big_x, small, small_c, small_1, small_x,
+    big, big_c, big_1, big_x, small, small_x,
     big_2, big_far, big_3, big_s, big_r, small_2, small_far, small_3, small_s, small_r,
     in_sem, out_sem, comm_sem,
     *, own, depth, hid, wide,
@@ -206,7 +206,10 @@
         lambda m: {"res": res_id(m // ns, ex, core), "seq": lax.rem(m, ns)},
         far_peer,
     )
-    greeted = (g_core, g_x, g_far)
+    g_xc = Group(
+        xn * cn, ex * cn + core, lambda m: {"res": res_id(wy, m // cn, lax.rem(m, cn))}
+    )
+    greeted = (g_xc, g_far)
     sems = Semaphores(comm_sem)
     loads = [
         pltpu.make_async_copy(a, b, in_sem.at[n])
@@ -546,7 +549,14 @@
     gl_t = mm3(split(gls_t), split(xs[...]))
     for h in range(2):
         small[:, h, :, :] = gl_t[:, h * wide : (h + 1) * wide].reshape(hid, 1, wide)
-    core_small = start_core(small, small_c, every)
+    def small_at(m):
+        return small.at[pl.ds(lax.rem(m, cn) * per_c + (m // cn) * per, per)]
+
+    xc_small = Exchange(
+        g_xc, sems, small_at, lambda k: small_x.at[k], small_x.at[: xn * cn - 1]
+    )
+    xc_small.start()
+    small_x[g_xc.me] = small_at(g_xc.me)[...]
 
     span_rows, span = far_chunk(per, g_far.size)
     groups = 8 // span
@@ -577,41 +587,44 @@
         at(whole, g_far.me)[...] = mine[...]
         return out
 
-    def red_at(red, c, x):
-        return red.at[pl.ds(c * per_c + x * per, per)]
-
-    def start_wide(exchange, whole, red):
+    def red_at(red, c, x, q):
+        return red.at[pl.ds(c * per_c + x * per, per), q]
+
+    def start_wide(exchange, whole, red, parts):
         exchange.wait_recv()
-        out = Exchange(
-            g_x, sems, lambda t: whole, lambda k: red_at(red, core, k),
-            red.at[: (xn - 1) * per], single=True,
-        )
-        out.start()
+        outs = []
+        for q in parts:
+            outs.append(
+                Exchange(
+                    g_x, sems, lambda t, q=q: whole.at[:, q],
+                    lambda k, q=q: red_at(red, core, k, q),
+                    red.at[: (xn - 1) * per, q], single=True,
+                )
+            )
+            outs[-1].start()
         mate = Exchange(
-            g_core, sems, lambda t: whole, lambda k: red_at(red, k, ex), red.at[: xn * per]
+            g_core, sems, lambda t: whole, lambda k: red_at(red, k, ex, every), red.at[: xn * per]
         )
         mate.start()
-        red_at(red, core, ex)[...] = whole[...]
-        return out, mate
-
-    def start_mates(wide_pair, red):
-        out, mate = wide_pair
-        for x in steps:
-            out.wait_from(x)
-            Exchange(
-                g_core,
-                sems,
-                lambda t, x=x: red_at(red, core, x),
-                lambda k, x=x: red_at(red, k, x),
-                share=mate,
-            ).start()
-
+        red_at(red, core, ex, every)[...] = whole[...]
+        return outs, mate
+
+    def start_mates(outs, mate, red, parts):
+        for out, q in zip(outs, parts):
+            for x in steps:
+                out.wait_from(x)
+                Exchange(
+                    g_core,
+                    sems,
+                    lambda t, x=x, q=q: red_at(red, core, x, q),
+                    lambda k, x=x, q=q: red_at(red, k, x, q),
+                    share=mate,
+                ).start()
+
+    far_big = start_far(x_big, big_x, big_2, big_far)
     up[...] = mm3(split(gls_t.T), wl_ts)
     norm_back(up, xs, xs_inv, rows_out, own, depth)
     store(rows_out, rows_res)
-    fold_core(core_small, small, small_c, small_1, every)
-    x_small = start_x(small_1, small_x, every)
-    far_big = start_far(x_big, big_x, big_2, big_far)
 
     x_edge.wait_recv()
     edge = edge_in[0]
@@ -621,27 +634,27 @@
         edge_out[pl.ds(j, own, stride=own), :] = edge[:, j * wide : (j + 1) * wide] + bias[...]
     store(edge_out, edge_res)
 
-    far_small = start_far([x_small], small_x, small_2, small_far)
+    far_small = start_far([xc_small], small_x, small_2, small_far)
     back_big = start_back(far_big, big_far, big_3, big_s)
     for sent in (
         x_cot, left_xs, left_ys, left_own, *left_far, first_gls, *x_gls, y_gls, x_edge,
-        *core_big, core_small, *x_big, x_small, far_big,
+        *core_big, xc_small, *x_big, far_big,
     ):
         sent.wait_send()
     back_small = start_back(far_small, small_far, small_3, small_s)
-    wide_big = start_wide(back_big, big_s, big_r)
-    start_mates(wide_big, big_r)
-    wide_small = start_wide(back_small, small_s, small_r)
-    wide_big[1].wait_recv()
+    wide_big, mate_big = start_wide(back_big, big_s, big_r, halves)
+    start_mates(wide_big, mate_big, big_r, halves)
+    wide_small, mate_small = start_wide(back_small, small_s, small_r, [every])
+    start_mates(wide_small, mate_small, small_r, [every])
+    mate_big.wait_recv()
     for h in range(hid):
         fin_out[h * hid : (h + 1) * hid, :] = big_r[
             :, h // 4, :, (h % 4) * wide : (h % 4 + 1) * wide
         ].reshape(hid, wide)
     store(fin_out, fin_res)
-    start_mates(wide_small, small_r)
-    for sent in (far_small, back_big, back_small, *wide_big):
+    for sent in (far_small, back_big, back_small, *wide_big, mate_big):
         sent.wait_send()
-    wide_small[1].wait_recv()
+    mate_small.wait_recv()
     for h in range(2):
         lanes = slice(h * wide, (h + 1) * wide)
         gl_out[:, lanes] = small_r[:, h].reshape(hid, wide)
@@ -650,7 +663,7 @@
     store(gl_out, gl_res)
     store(gr_out, gr_res)
     store(gb_out, gb_res)
-    for sent in wide_small:
+    for sent in (*wide_small, mate_small):
         sent.wait_send()
     for put in stores:
         put.wait()
@@ -737,8 +750,7 @@
         v((flat, hid), F32), v((flat, chan), F32),
         v((hid, 8, 1, 4 * wide), F32), v((per_c, 8, 1, 4 * wide), F32),
         v((per_c, 8, 1, 4 * wide), F32), v((xn, per, 8, 1, 4 * wide), F32),
-        v((hid, 8, 1, wide), F32), v((per_c, 8, 1, wide), F32),
-        v((per_c, 8, 1, wide), F32), v((xn, per, 8, 1, wide), F32),
+        v((hid, 8, 1, wide), F32), v((xn * cn, per, 8, 1, wide), F32),
     ]
     for lanes in (4 * wide, wide):
         scratch += [

time: 69.3 us -> 68.8 us (level)
  no operation moved by 1% of the time
where the time goes in v6:
time: 68.8 us; the launch traced here: 68.7 us
  Pallas kernels  68 us (99%)
    pallas_call x1, Pallas kernels, body(): pl.pallas_call(functools.partial(kernel, own=own, depth=depth, hid=hid, w...  66.8 us

profile of v6, /device:TPU:1, one launch (start us, length us, event | category | flops | bytes accessed | tf_op | source)
XLA Modules:
  0.0 68.7 jit_solution(14791479326931866124)
XLA Ops:
  0.6 66.8 %outer_mean.1 = (f32[64,128]{1,0:T(8,128)S(1)}, f32[1024,128]{1,0:T(8,128)S(1)}, f32[1024,128]{1,0:T(8,128)S(1)}, f32[1024,128]{1,0:T(8,128)S(1)}, f32[32,256]{1...) custom-call(f32[1024,128]{1,0:T(8,128)} %bitcast.28, f32[1024,128]{1,0:T(8,128)} %bitcast.29, ...), custom_call_target="tpu_custom_call" | custom-call | tf_op jit(solution)/shard_map/outer_mean/pallas_call | solution.py:767
  67.4 1.2 %copy_out.1 = (f32[64,128]{1,0:T(8,128)}, f32[1024,128]{1,0:T(8,128)}, f32[1024,128]{1,0:T(8,128)}, f32[1024,128]{1,0:T(8,128)}, f32[32,256]{1,0:T(8,128)}, /*index=5*/f32[32,256]{1,0:T(8,128)}, f32[1,128]{1,0:T(1,128)}) custom-call(f32[64,128]{1,0:T(8,128)S(1)} %get-tuple-element.21.refs_0_, f32[1024,128]{1,0:T(8,128)S(1)} %get-tuple-element.22.refs_1_, ...), custom_call_target="tpu_custom_call" | custom-call | tf_op jit(solution)/shard_map/copy_out/pallas_call | solution.py:686
